TPU v7x, 32 devices: a whole 2x2x4 slice. The times are simulated.
32 devices in a mesh: dp: 2 (over core), expert: 16 (over z, y, x).
Axes of the slice: x: 2, y: 2, z: 4, core: 2. Of those that a mesh axis runs over, the one named last changes fastest.
Arguments:
- weights: bfloat16 [4, 3584, 512], P(None, ('dp', 'expert')), may hold values from -0.09375 to 0.09375
- first_moment: float32 [4, 3584, 512], P(None, ('dp', 'expert')), may hold values from -3 to 3
- second_moment: float32 [4, 3584, 512], P(None, ('dp', 'expert')), may hold values from 0.05 to 2
- placement: int32 [16], replicated, may hold values from 0 to 3, as said below
- block_counts: int32 [2, 16], P('dp', 'expert'), may hold values from 1 to 2
- tokens: bfloat16 [2, 16, 256, 3584], P('dp', 'expert'), may hold values from -6 to 6
- hidden_grad: bfloat16 [2, 16, 256, 256], P('dp', 'expert'), may hold values from -1.1953125 to 1.1953125
Outputs:
- new_weights: bfloat16 [16, 3584, 512], P('expert', 'dp')
- new_first: float32 [16, 3584, 512], P('expert', 'dp')
- new_second: float32 [16, 3584, 512], P('expert', 'dp')
Inputs may be any that keep to these rules, and one draw needn't show every extreme that they name: `placement`: every expert block 0 to 3 is owned by at least one device. `block_counts`: the rows after a device's live blocks are padding.
All inputs are finite; a program needn't handle non-finite values.
Results may differ from a plain program's by a relative error of at most 0.015.
Values may be sent and summed in bfloat16 or wider, within the bound.
A program may use at most 64 MiB of HBM per device.

v0:
```python
import jax
import jax.numpy as jnp
from jax import lax
from jax.sharding import PartitionSpec as P

BLOCK = 128


beta_first = 0.9
beta_second = 0.95
learning_rate = 0.001
weight_decay = 0.1
adam_epsilon = 1e-08
adam_steps = 10.0


def silu_grads(projected, upstream, live_mask):
    half_width = projected.shape[1] // 2
    gate_part = projected[:, :half_width]
    upward = projected[:, half_width:]
    sigmoid_gate = jax.nn.sigmoid(gate_part)
    masked = jnp.where(live_mask, upstream.astype(jnp.float32), 0.0)
    grad_gate = masked * upward * sigmoid_gate * (1.0 + gate_part * (1.0 - sigmoid_gate))
    grad_upward = masked * gate_part * sigmoid_gate
    return jnp.concatenate([grad_gate, grad_upward], axis=1).astype(jnp.bfloat16)


def adam_update(params, first_moment, second_moment, gradient):
    moment_one = beta_first * first_moment + (1.0 - beta_first) * gradient
    moment_two = beta_second * second_moment + (1.0 - beta_second) * gradient * gradient
    correct_one = 1.0 - beta_first**adam_steps
    correct_two = 1.0 - beta_second**adam_steps
    params_full = params.astype(jnp.float32)
    step_size = (
        moment_one / correct_one / (jnp.sqrt(moment_two / correct_two) + adam_epsilon)
        + weight_decay * params_full
    )
    return ((params_full - learning_rate * step_size).astype(jnp.bfloat16), moment_one, moment_two)


def on_device(weights, first_moment, second_moment, placement, block_counts, tokens, hidden_grad):
    expert_count = lax.axis_size("expert")
    dp_count = lax.axis_size("dp")
    block_total = weights.shape[0]
    span_rows = weights.shape[1]
    col_total = weights.shape[2]
    inputs = tokens[0, 0]
    row_total = inputs.shape[0]
    owner_table = (placement[:, None] == jnp.arange(block_total)[None, :]).astype(jnp.float32)
    live_mask = (jnp.arange(row_total) < BLOCK * block_counts[0, 0])[:, None]
    outgoing = jnp.take(weights, placement, axis=0)
    arrived = lax.all_to_all(outgoing, "expert", split_axis=0, concat_axis=0, tiled=True)
    own_rows = arrived.reshape(expert_count * span_rows, col_total)
    projected = jnp.dot(
        inputs,
        lax.all_gather(own_rows, "dp", axis=0, tiled=True),
        preferred_element_type=jnp.float32,
    )
    grad_proj = silu_grads(projected, hidden_grad[0, 0], live_mask)
    split_inputs = inputs.reshape(row_total, dp_count, expert_count, span_rows)
    full_grad = jnp.einsum(
        "tice,tf->cief", split_inputs, grad_proj, preferred_element_type=jnp.float32
    ).astype(jnp.bfloat16)
    at_home = lax.all_to_all(full_grad, "expert", split_axis=0, concat_axis=0, tiled=True)
    by_block = lax.dot_general(
        owner_table.astype(jnp.bfloat16),
        at_home.reshape(expert_count, dp_count * span_rows * col_total),
        (((0,), (0,)), ((), ())),
        preferred_element_type=jnp.float32,
    )
    by_block = by_block.reshape(block_total, dp_count, span_rows, col_total)
    block_grad = lax.psum_scatter(by_block, "dp", scatter_dimension=1, tiled=True).reshape(
        block_total, span_rows, col_total
    )
    first_sent = jnp.take(first_moment, placement, axis=0)
    second_sent = jnp.take(second_moment, placement, axis=0)
    grad_sent = jnp.take(block_grad, placement, axis=0)
    first_here, second_here, grad_here = (
        lax.all_to_all(first_sent, "expert", split_axis=0, concat_axis=0, tiled=True),
        lax.all_to_all(second_sent, "expert", split_axis=0, concat_axis=0, tiled=True),
        lax.all_to_all(grad_sent, "expert", split_axis=0, concat_axis=0, tiled=True),
    )
    own_shape = (expert_count * span_rows, col_total)
    updated, moment_one, moment_two = adam_update(
        own_rows,
        first_here.reshape(own_shape),
        second_here.reshape(own_shape),
        grad_here.reshape(own_shape),
    )
    return (updated[None], moment_one[None], moment_two[None])


def solution(mesh):
    in_specs = (
        P(None, ("dp", "expert"), None),
        P(None, ("dp", "expert"), None),
        P(None, ("dp", "expert"), None),
        P(),
        P("dp", "expert"),
        P("dp", "expert", None, None),
        P("dp", "expert", None, None),
    )
    out_specs = (P("expert", "dp", None), P("expert", "dp", None), P("expert", "dp", None))
    return jax.shard_map(
        on_device, mesh=mesh, in_specs=in_specs, out_specs=out_specs, check_vma=False
    )
```

profile of v0, /device:TPU:12, one launch (start us, length us, event | category | flops | bytes accessed | tf_op | source)
XLA Modules:
  0.0 470.6 jit_solution(14140576036881196201)
XLA Ops:
  7.2 0.0 copy-start
  7.2 0.0 all-gather.2.cloned.1.call-start
  7.2 0.8 compare_and_fusion
  8.0 0.7 compare_select_fusion
  8.7 2.9 gather_fusion
  11.6 1.7 broadcast_select_fusion.3
  13.3 0.0 copy-start.5
  13.3 49.2 %all_to_all.25 = bf16[16,112,512]{2,1,0:T(8,128)(2,1)} all-to-all(bf16[16,112,512]{2,1,0:T(8,128)(2,1)S(1)} %broadcast_select_fusion.3), channel_id=1, replica_groups=mesh['dp'=2,'expert'=16] {'expert'}, dimensions={0} | all-to-all | bytes 3670016 | tf_op jit(solution)/shard_map/all_to_all | solution.py:52
  62.6 0.0 all-gather.2.cloned.1.call-update
  62.6 0.0 reduce-scatter.2.cloned.1.call-start
  63.3 0.0 copy-done.5
  63.3 0.1 copy.19
  63.4 11.5 %all-gather.2.cloned.1.call-done = bf16[3584,512]{1,0:T(8,128)(2,1)} async-done(((bf16[1792,512]{1,0:T(8,128)(2,1)}), bf16[3584,512]{1,0:T(8,128)(2,1)}) %all-gather.2.cloned.1.call-update) | async-done | bytes 3670032 | tf_op jit(solution)/shard_map/all_gather | solution.py:56
  75.0 0.0 copy-done
  75.0 3.2 fusion.11
  78.2 0.2 fusion.16
  78.3 1.2 fusion.7
  79.5 0.6 convert_bitcast_fusion
  80.1 0.2 copy.22
  80.3 0.0 copy-start.6
  80.3 88.5 %all_to_all.26 = bf16[16,2,112,512]{3,2,1,0:T(8,128)(2,1)S(1)} all-to-all(bf16[16,2,112,512]{3,2,1,0:T(8,128)(2,1)S(1)} %copy.22), channel_id=1, replica_groups=mesh['dp'=2,'expert'=16] {'expert'}, dimensions={0} | all-to-all | bytes 7340032 | tf_op jit(solution)/shard_map/all_to_all | solution.py:64
  168.9 0.0 copy-done.6
  168.9 2.2 fusion.5
  171.1 0.0 copy-start.3
  171.1 1.8 copy.24
  172.9 0.0 reduce-scatter.2.cloned.1.call-update
  172.9 0.0 copy-done.3
  172.9 0.0 copy-start.4
  172.9 2.6 gather_fusion.3
  175.5 0.0 copy-done.4
  175.5 2.6 gather_fusion.1
  178.2 3.7 reduce-scatter.2.cloned.1.call-done
  181.9 3.8 gather_fusion.2
  185.6 8.5 %broadcast_select_fusion = (f32[16,112,512]{2,1,0:T(8,128)S(1)}, f32[16,112,512]{2,1,0:T(8,128)S(1)}, f32[16,112,512]{2,1,0:T(8,128)}) fusion(f32[16,112,512]{2,1,0:T(8,128)} %gather_fusion.3, pred[16]{0:T(512)(128)(4,1)S(1)} %compare_and_fusion, f32[16,112,512]{2,1,0:T(8,128)} %gather_fusion.1, f32[16,112,512]{2,1,0:T(8,128)} %gather_fusion.2), kind=kLoop, calls=%fused_computation.20 | loop fusion | flops 2752512 | bytes 22020112 | tf_op jit(solution)/shard_map/jit(_take)/select_n | solution.py:76
  194.1 88.5 %all_to_all.27 = f32[16,112,512]{2,1,0:T(8,128)} all-to-all(f32[16,112,512]{2,1,0:T(8,128)S(1)} %get-tuple-element.9), channel_id=1, replica_groups=mesh['dp'=2,'expert'=16] {'expert'}, dimensions={0} | all-to-all | bytes 7340032 | tf_op jit(solution)/shard_map/all_to_all | solution.py:80
  282.6 85.8 %all_to_all.28 = f32[16,112,512]{2,1,0:T(8,128)} all-to-all(f32[16,112,512]{2,1,0:T(8,128)S(1)} %get-tuple-element.10), channel_id=1, replica_groups=mesh['dp'=2,'expert'=16] {'expert'}, dimensions={0} | all-to-all | bytes 7340032 | tf_op jit(solution)/shard_map/all_to_all | solution.py:79
  368.5 5.6 %all-to-all-start.3 = ((f32[16,112,512]{2,1,0:T(8,128)}), f32[16,112,512]{2,1,0:T(8,128)}, u32[]{:S(2)}, u32[]{:S(2)}) async-start(f32[16,112,512]{2,1,0:T(8,128)} %get-tuple-element.11), calls=%async_computation.4 | async-start | bytes 7340032 | tf_op jit(solution)/shard_map/all_to_all | solution.py:81
  374.0 0.0 copy-start.2
  374.0 4.6 broadcast_multiply_fusion
  378.6 0.0 copy-done.2
  378.6 2.3 broadcast_multiply_fusion.1
  380.9 74.0 %all-to-all-done.3 = f32[16,112,512]{2,1,0:T(8,128)} async-done(((f32[16,112,512]{2,1,0:T(8,128)}), f32[16,112,512]{2,1,0:T(8,128)}, u32[]{:S(2)}, u32[]{:S(2)}) %all-to-all-start.3) | async-done | bytes 3670048 | tf_op jit(solution)/shard_map/all_to_all | solution.py:81
  455.0 0.0 copy-start.1
  455.0 8.8 %fusion.2 = (bf16[1,1792,512]{2,1,0:T(8,128)(2,1)}, f32[1,1792,512]{2,1,0:T(8,128)}, f32[1,1792,512]{2,1,0:T(8,128)}) fusion(bf16[1,1792,512]{2,1,0:T(8,128)(2,1)} %bitcast.59, f32[1,1792,512]{2,1,0:T(8,128)} %bitcast.51.clone.2, f32[1,1792,512]{2,1,0:T(8,128)} %bitcast.63, f32[1,1792,512]{2,1,0:T(8,128)} %bitcast.62), kind=kLoop, calls=%fused_computation.9 | loop fusion | flops 13762560 | bytes 22020096 | tf_op jit(solution)/shard_map/convert_element_type | solution.py:38
  463.8 0.0 copy-done.1
  (2 shorter events, 0.0 us)
Async XLA Ops:
  7.2 67.8 %copy-start = (bf16[1,1,256,3584]{3,2,1,0:T(8,128)(2,1)S(1)}, bf16[1,1,256,3584]{3,2,1,0:T(8,128)(2,1)}, u32[]{:S(2)}) copy-start(bf16[1,1,256,3584]{3,2,1,0:T(8,128)(2,1)} %param.14) | copy-start | bytes 5505028
  7.2 67.8 %all-gather.2.cloned.1.call-start = ((), (), s32[]{:S(2)}) async-start(), calls=%async_computation.6 | async-start | bytes 5505024 | tf_op jit(solution)/shard_map/all_gather | solution.py:56
  13.3 49.9 %copy-start.5 = (bf16[1,1,256,256]{3,2,1,0:T(8,128)(2,1)S(1)}, bf16[1,1,256,256]{3,2,1,0:T(8,128)(2,1)}, u32[]{:S(2)}) copy-start(bf16[1,1,256,256]{3,2,1,0:T(8,128)(2,1)} %param.15) | copy-start | bytes 393220
  62.6 119.3 %reduce-scatter.2.cloned.1.call-start = ((), (), s32[]{:S(2)}) async-start(), calls=%async_computation.7 | async-start | bytes 2752512 | tf_op jit(solution)/shard_map/reduce_scatter | solution.py:72
  80.3 88.6 %copy-start.6 = (s32[16]{0:T(128)S(1)}, s32[16]{0:T(128)}, u32[]{:S(2)}) copy-start(s32[16]{0:T(128)} %param.12) | copy-start | bytes 196
  171.1 1.8 copy-start.3
  172.9 2.6 copy-start.4
  368.5 86.5 %all-to-all-start.3 = ((f32[16,112,512]{2,1,0:T(8,128)}), f32[16,112,512]{2,1,0:T(8,128)}, u32[]{:S(2)}, u32[]{:S(2)}) async-start(f32[16,112,512]{2,1,0:T(8,128)} %get-tuple-element.11), calls=%async_computation.4 | async-start | bytes 7340032 | tf_op jit(solution)/shard_map/all_to_all | solution.py:81
  374.0 4.6 copy-start.2
  455.0 8.8 %copy-start.1 = (bf16[1,1,256,3584]{3,2,1,0:T(8,128)(2,1)S(1)}, bf16[1,1,256,3584]{3,2,1,0:T(8,128)(2,1)}, u32[]{:S(2)}) copy-start(bf16[1,1,256,3584]{3,2,1,0:T(8,128)(2,1)} %param.14) | copy-start | bytes 5505028
Sparse Core Ops, SparseCore 0:
  62.7 12.2 all-gather.1
  173.0 8.8 reduce-scatter.1
where the time goes:
time: 471 us
  blocking collectives  312 us (66%)
  waiting for transfers between devices  89.3 us (19%)
  other arithmetic  28.1 us (6%)
  between operations  14.8 us (3%)
  local copies, waits for them, and re-layouts  14.1 us (3%)
  matrix products  6.57 us (1%)
  starting transfers between devices  5.67 us (1%)
    all_to_all x1, blocking collectives, on_device(): lax.all_to_all(full_grad, 'expert', split_axis=0, concat_axis=0, tiled=True)  88.5 us
    all_to_all x1, blocking collectives, on_device(): lax.all_to_all(second_sent, 'expert', split_axis=0, concat_axis=0, tiled=...  88.5 us
    all_to_all x1, blocking collectives, on_device(): lax.all_to_all(first_sent, 'expert', split_axis=0, concat_axis=0, tiled=T...  85.8 us
    all_to_all x1, waiting for transfers between devices, on_device(): lax.all_to_all(grad_sent, 'expert', split_axis=0, concat_axis=0, tiled=True)  74 us
    all_to_all x1, blocking collectives, on_device(): lax.all_to_all(outgoing, 'expert', split_axis=0, concat_axis=0, tiled=True)  49.2 us
    all_gather x1, waiting for transfers between devices, on_device(): lax.all_gather(own_rows, 'dp', axis=0, tiled=True)  11.5 us
  transfers between devices with their start and end apart: 3, of which 3 were waited for; matrix products, arithmetic and copies ran while one was open for 3% of the time, Pallas kernels for 0%

commit v1 on v0

v1 whole, which is shorter than its diff:
```python
import jax
import jax.numpy as jnp
from jax import lax
from jax.sharding import PartitionSpec as P

BLOCK = 128


beta_first = 0.9
beta_second = 0.95
learning_rate = 0.001
weight_decay = 0.1
adam_epsilon = 1e-08
adam_steps = 10.0


def silu_grads(projected, upstream, live_mask):
    half_width = projected.shape[1] // 2
    gate_part = projected[:, :half_width]
    upward = projected[:, half_width:]
    sigmoid_gate = jax.nn.sigmoid(gate_part)
    masked = jnp.where(live_mask, upstream.astype(jnp.float32), 0.0)
    grad_gate = masked * upward * sigmoid_gate * (1.0 + gate_part * (1.0 - sigmoid_gate))
    grad_upward = masked * gate_part * sigmoid_gate
    return jnp.concatenate([grad_gate, grad_upward], axis=1).astype(jnp.bfloat16)


def moments(first_moment, second_moment, gradient):
    moment_one = beta_first * first_moment + (1.0 - beta_first) * gradient
    moment_two = beta_second * second_moment + (1.0 - beta_second) * gradient * gradient
    return moment_one, moment_two


def new_params(params, moment_one, moment_two):
    correct_one = 1.0 - beta_first**adam_steps
    correct_two = 1.0 - beta_second**adam_steps
    params_full = params.astype(jnp.float32)
    step_size = (
        moment_one / correct_one / (jnp.sqrt(moment_two / correct_two) + adam_epsilon)
        + weight_decay * params_full
    )
    return (params_full - learning_rate * step_size).astype(jnp.bfloat16)


def exchange(x, axis):
    return lax.all_to_all(x, axis, split_axis=0, concat_axis=0, tiled=True)


def on_device(weights, first_moment, second_moment, placement, block_counts, tokens, hidden_grad):
    expert_count = lax.axis_size("expert")
    dp_count = lax.axis_size("dp")
    block_total, span_rows, col_total = weights.shape
    row_total = tokens.shape[2]
    part_rows = expert_count * span_rows
    owner_table = (placement[:, None] == jnp.arange(block_total)[None, :]).astype(jnp.bfloat16)
    live_mask = (jnp.arange(row_total) < BLOCK * block_counts[0, 0])[:, None]

    own_rows = exchange(jnp.take(weights, placement, axis=0), "expert")
    own_rows = own_rows.reshape(part_rows, col_total)
    inputs = lax.all_to_all(tokens[0, 0], "dp", split_axis=1, concat_axis=0, tiled=True)
    partial = jnp.dot(inputs, own_rows, preferred_element_type=jnp.float32)
    projected = lax.psum_scatter(partial, "dp", scatter_dimension=0, tiled=True)
    grad_proj = silu_grads(projected, hidden_grad[0, 0], live_mask)
    grad_proj = lax.all_gather(grad_proj, "dp", axis=0, tiled=True)
    term = lax.dot_general(
        inputs, grad_proj, (((0,), (0,)), ((), ())), preferred_element_type=jnp.float32
    ).astype(jnp.bfloat16)
    at_home = exchange(term.reshape(expert_count, span_rows * col_total), "expert")
    block_grad = lax.dot_general(
        owner_table, at_home, (((0,), (0,)), ((), ())), preferred_element_type=jnp.float32
    ).reshape(block_total, span_rows, col_total)
    moment_one, moment_two = moments(first_moment, second_moment, block_grad)
    one_here = exchange(jnp.take(moment_one.astype(jnp.bfloat16), placement, axis=0), "expert")
    two_here = exchange(jnp.take(moment_two.astype(jnp.bfloat16), placement, axis=0), "expert")
    one_here = one_here.reshape(part_rows, col_total).astype(jnp.float32)
    two_here = two_here.reshape(part_rows, col_total).astype(jnp.float32)
    updated = new_params(own_rows, one_here, two_here)
    return (updated[None], one_here[None], two_here[None])


def solution(mesh):
    in_specs = (
        P(None, ("dp", "expert"), None),
        P(None, ("dp", "expert"), None),
        P(None, ("dp", "expert"), None),
        P(),
        P("dp", "expert"),
        P("dp", "expert", None, None),
        P("dp", "expert", None, None),
    )
    out_specs = (P("expert", "dp", None), P("expert", "dp", None), P("expert", "dp", None))
    return jax.shard_map(
        on_device, mesh=mesh, in_specs=in_specs, out_specs=out_specs, check_vma=False
    )
```

time: 471 us -> 298 us (0.63)
  the two profiles are of different devices: /device:TPU:12 before, /device:TPU:0 now
where the time goes in v1:
time: 298 us; the launch traced here: 297 us
  blocking collectives  146 us (49%)
  waiting for transfers between devices  46.6 us (16%)
  local copies, waits for them, and re-layouts  44.2 us (15%)
  other arithmetic  26.4 us (9%)
  between operations  14.8 us (5%)
  starting transfers between devices  12.2 us (4%)
  matrix products  6.41 us (2%)
    all_to_all x3, blocking collectives, exchange(): return lax.all_to_all(x, axis, split_axis=0, concat_axis=0, tiled=True)  144 us
    all_to_all x1, waiting for transfers between devices, exchange(): return lax.all_to_all(x, axis, split_axis=0, concat_axis=0, tiled=True)  35 us
    unnamed x19, local copies, waits for them, and re-layouts  24.1 us
    all_to_all x1, other arithmetic, exchange(): return lax.all_to_all(x, axis, split_axis=0, concat_axis=0, tiled=True)  13.6 us
    reduce_scatter x1, waiting for transfers between devices, on_device(): projected = lax.psum_scatter(partial, 'dp', scatter_dimension=0, tiled=True)  11.6 us
    all_to_all x1, starting transfers between devices, exchange(): return lax.all_to_all(x, axis, split_axis=0, concat_axis=0, tiled=True)  8.34 us
    all_to_all x2, local copies, waits for them, and re-layouts, exchange(): return lax.all_to_all(x, axis, split_axis=0, concat_axis=0, tiled=True)  6.72 us
  transfers between devices with their start and end apart: 3, of which 2 were waited for; matrix products, arithmetic and copies ran while one was open for 3% of the time, Pallas kernels for 0%

profile of v1, /device:TPU:0, one launch (start us, length us, event | category | flops | bytes accessed | tf_op | source)
XLA Modules:
  0.0 296.7 jit_solution(797748564461970987)
XLA Ops:
  7.2 0.0 copy-start
  7.2 3.9 %copy.40 = bf16[1,1,256,3584]{2,3,1,0:T(8,128)(2,1)} copy(bf16[1,1,256,3584]{3,2,1,0:T(8,128)(2,1)} %param.14) | data formatting | bytes 3670016 | tf_op args[5]
  11.0 0.0 copy-start.6
  11.0 3.9 %all-to-all-start.1 = ((bf16[256,2,1792]{0,2,1:T(8,128)(2,1)}), bf16[256,2,1792]{0,2,1:T(8,128)(2,1)S(1)}, u32[]{:S(2)}, u32[]{:S(2)}) async-start(bf16[256,2,1792]{0,2,1:T(8,128)(2,1)} %bitcast.44), calls=%async_computation.1 | async-start | bytes 3670016 | tf_op jit(solution)/shard_map/all_to_all | solution.py:60
  14.9 0.0 copy-done.6
  14.9 0.0 copy-done
  15.0 1.9 gather_fusion
  16.8 3.0 %broadcast_select_fusion.2 = bf16[16,112,512]{2,1,0:T(8,128)(2,1)} fusion(bf16[16,112,512]{2,1,0:T(8,128)(2,1)} %gather_fusion, pred[16]{0:T(512)(128)(4,1)S(1)} %compare_and_fusion), kind=kLoop, calls=%fused_computation.17 | loop fusion | flops 917504 | bytes 3670032 | tf_op jit(solution)/shard_map/jit(_take)/select_n | solution.py:58
  19.8 0.0 all-to-all-done.1
  19.8 0.0 copy-start.1
  19.8 1.2 copy-done.1
  21.0 8.3 %all-to-all-start = ((bf16[16,112,512]{2,1,0:T(8,128)(2,1)}), bf16[16,112,512]{2,1,0:T(8,128)(2,1)S(1)}, u32[]{:S(2)}, u32[]{:S(2)}) async-start(bf16[16,112,512]{2,1,0:T(8,128)(2,1)} %broadcast_select_fusion.2), calls=%async_computation | async-start | bytes 3670016 | tf_op jit(solution)/shard_map/all_to_all | solution.py:46
  29.4 0.0 reduce-scatter.2.cloned.1.call-start
  29.4 3.8 %copy.41 = bf16[2,256,1792]{2,1,0:T(8,128)(2,1)} copy(bf16[2,256,1792]{1,2,0:T(8,128)(2,1)} %bitcast.43) | data formatting | bytes 3670016 | tf_op jit(solution)/shard_map/all_to_all | solution.py:60
  33.3 35.0 %all-to-all-done = bf16[16,112,512]{2,1,0:T(8,128)(2,1)S(1)} async-done(((bf16[16,112,512]{2,1,0:T(8,128)(2,1)}), bf16[16,112,512]{2,1,0:T(8,128)(2,1)S(1)}, u32[]{:S(2)}, u32[]{:S(2)}) %all-to-all-start) | async-done | bytes 1835040 | tf_op jit(solution)/shard_map/all_to_all | solution.py:46
  68.3 0.0 copy-start.5
  68.3 3.7 %convolution_bitcast_fusion = f32[512,512]{0,1:T(8,128)} fusion(bf16[1792,512]{1,0:T(8,128)(2,1)S(1)} %bitcast.39, bf16[512,1792]{1,0:T(8,128)(2,1)} %bitcast.46), kind=kOutput, calls=%fused_computation.19 | convolution fusion | flops 939524096 | bytes 4718592 | tf_op jit(solution)/shard_map/dot_general | solution.py:61
  72.0 0.0 reduce-scatter.2.cloned.1.call-update
  72.6 0.0 copy-done.5
  72.6 0.1 copy.39
  72.8 11.6 %reduce-scatter.2.cloned.1.call-done = f32[256,512]{0,1:T(8,128)} async-done(((f32[512,512]{0,1:T(8,128)}), f32[256,512]{0,1:T(8,128)}) %reduce-scatter.2.cloned.1.call-update) | async-done | bytes 524304 | tf_op jit(solution)/shard_map/reduce_scatter | solution.py:62
  84.3 0.0 copy-start.2
  84.3 1.3 fusion.11
  85.6 2.2 all_gather.3
  87.8 0.0 copy-done.2
  87.8 2.3 fusion.3
  90.2 3.8 %copy.42 = bf16[1792,512]{1,0:T(8,128)(2,1)} copy(bf16[1792,512]{0,1:T(8,128)(2,1)} %fusion.3) | data formatting | bytes 3670016 | tf_op jit(solution)/shard_map/convert_element_type | solution.py:67
  94.0 6.2 %all_to_all.41 = bf16[16,1,57344]{2,1,0:T(2,128)(2,1)} reshape(bf16[1792,512]{1,0:T(8,128)(2,1)} %copy.42) | data formatting | bytes 3670016 | tf_op jit(solution)/shard_map/all_to_all | solution.py:46
  100.2 0.5 broadcast.92
  100.7 13.6 %reduce = bf16[16,57344]{1,0:T(8,128)(2,1)} reduce(bf16[16,1,57344]{2,1,0:T(2,128)(2,1)} %all_to_all.41, bf16[]{:T(256)} %broadcast.92), dimensions={1}, to_apply=%all_to_all.41.reduce_sub_computation | reduce | bytes 3670018 | tf_op jit(solution)/shard_map/all_to_all | solution.py:46
  114.3 3.6 %reshape.148 = bf16[16,2,28672]{2,1,0:T(2,128)(2,1)} reshape(bf16[16,57344]{1,0:T(8,128)(2,1)} %reduce) | data formatting | bytes 3670016
  117.9 51.1 %all_to_all.47 = bf16[16,2,28672]{2,1,0:T(2,128)(2,1)} all-to-all(bf16[16,2,28672]{2,1,0:T(2,128)(2,1)} %reshape.148), channel_id=1, replica_groups=mesh['dp'=2,'expert'=16] {'expert'}, dimensions={0} | all-to-all | bytes 3670016 | tf_op jit(solution)/shard_map/all_to_all | solution.py:46
  169.0 10.2 %reshape.149 = bf16[16,1,57344]{2,1,0:T(2,128)(2,1)} reshape(bf16[16,2,28672]{2,1,0:T(2,128)(2,1)} %all_to_all.47) | data formatting | bytes 3670016
  179.2 4.0 %copy.48 = bf16[16,1,57344]{2,0,1:T(8,128)(2,1)S(1)} copy(bf16[16,1,57344]{2,1,0:T(2,128)(2,1)} %reshape.149) | data formatting | bytes 3670016
  183.3 0.0 copy-start.3
  183.3 0.0 copy-start.4
  183.3 0.4 fusion.4
  183.7 0.8 copy-done.3
  184.5 0.3 copy-done.4
  184.7 0.6 fusion.8
  185.3 1.9 gather_fusion.2
  187.2 1.9 gather_fusion.1
  189.1 2.4 broadcast_select_fusion
  191.5 46.4 %all_to_all.48 = bf16[16,112,512]{2,1,0:T(8,128)(2,1)S(1)} all-to-all(bf16[16,112,512]{2,1,0:T(8,128)(2,1)S(1)} %get-tuple-element.11), channel_id=1, replica_groups=mesh['dp'=2,'expert'=16] {'expert'}, dimensions={0} | all-to-all | bytes 3670016 | tf_op jit(solution)/shard_map/all_to_all | solution.py:46
  237.9 46.4 %all_to_all.49 = bf16[16,112,512]{2,1,0:T(8,128)(2,1)S(1)} all-to-all(bf16[16,112,512]{2,1,0:T(8,128)(2,1)S(1)} %get-tuple-element.12), channel_id=1, replica_groups=mesh['dp'=2,'expert'=16] {'expert'}, dimensions={0} | all-to-all | bytes 3670016 | tf_op jit(solution)/shard_map/all_to_all | solution.py:46
  284.4 5.4 %fusion.2 = (bf16[1,1792,512]{2,1,0:T(8,128)(2,1)}, f32[1,1792,512]{2,1,0:T(8,128)}, f32[1,1792,512]{2,1,0:T(8,128)}) fusion(bf16[1,1792,512]{2,1,0:T(8,128)(2,1)S(1)} %bitcast.40, bf16[1,1792,512]{2,1,0:T(8,128)(2,1)S(1)} %bitcast.42, bf16[1,1792,512]{2,1,0:T(8,128)(2,1)S(1)} %bitcast.41), kind=kLoop, calls=%fused_computation.7 | loop fusion | flops 11010048 | bytes 14680064 | tf_op jit(solution)/shard_map/convert_element_type | solution.py:42
  (5 shorter events, 0.0 us)
Async XLA Ops:
  7.2 7.8 %copy-start = (bf16[4,112,512]{2,1,0:T(8,128)(2,1)S(1)}, bf16[4,112,512]{2,1,0:T(8,128)(2,1)}, u32[]{:S(2)}) copy-start(bf16[4,112,512]{2,1,0:T(8,128)(2,1)} %param.9) | copy-start | bytes 1376260
  11.0 3.9 %copy-start.6 = (s32[16]{0:T(128)S(1)}, s32[16]{0:T(128)}, u32[]{:S(2)}) copy-start(s32[16]{0:T(128)} %param.12) | copy-start | bytes 196
  11.0 8.8 %all-to-all-start.1 = ((bf16[256,2,1792]{0,2,1:T(8,128)(2,1)}), bf16[256,2,1792]{0,2,1:T(8,128)(2,1)S(1)}, u32[]{:S(2)}, u32[]{:S(2)}) async-start(bf16[256,2,1792]{0,2,1:T(8,128)(2,1)} %bitcast.44), calls=%async_computation.1 | async-start | bytes 3670016 | tf_op jit(solution)/shard_map/all_to_all | solution.py:60
  19.8 1.2 copy-start.1
  21.0 47.2 %all-to-all-start = ((bf16[16,112,512]{2,1,0:T(8,128)(2,1)}), bf16[16,112,512]{2,1,0:T(8,128)(2,1)S(1)}, u32[]{:S(2)}, u32[]{:S(2)}) async-start(bf16[16,112,512]{2,1,0:T(8,128)(2,1)} %broadcast_select_fusion.2), calls=%async_computation | async-start | bytes 3670016 | tf_op jit(solution)/shard_map/all_to_all | solution.py:46
  29.4 54.9 %reduce-scatter.2.cloned.1.call-start = ((), (), s32[]{:S(2)}) async-start(), calls=%async_computation.6 | async-start | bytes 1572864 | tf_op jit(solution)/shard_map/reduce_scatter | solution.py:62
  68.3 4.3 %copy-start.5 = (bf16[1,1,256,256]{3,2,1,0:T(8,128)(2,1)S(1)}, bf16[1,1,256,256]{3,2,1,0:T(8,128)(2,1)}, u32[]{:S(2)}) copy-start(bf16[1,1,256,256]{3,2,1,0:T(8,128)(2,1)} %param.15) | copy-start | bytes 393220
  84.3 3.5 %copy-start.2 = (bf16[2,256,1792]{2,1,0:T(8,128)(2,1)S(1)}, bf16[2,256,1792]{2,1,0:T(8,128)(2,1)}, u32[]{:S(2)}) copy-start(bf16[2,256,1792]{2,1,0:T(8,128)(2,1)} %copy.41) | copy-start | bytes 5505028
  183.3 1.2 copy-start.3
  183.3 1.4 copy-start.4
Sparse Core Ops, SparseCore 0:
  72.1 12.1 reduce-scatter.1

commit v2 on v1

--- a/solution.py
+++ b/solution.py
@@ -1,6 +1,10 @@
+import functools
+
 import jax
 import jax.numpy as jnp
 from jax import lax
+from jax.experimental import pallas as pl
+from jax.experimental.pallas import tpu as pltpu
 from jax.sharding import PartitionSpec as P
 
 BLOCK = 128
@@ -46,7 +50,7 @@
     return lax.all_to_all(x, axis, split_axis=0, concat_axis=0, tiled=True)
 
 
-def on_device(weights, first_moment, second_moment, placement, block_counts, tokens, hidden_grad):
+def on_device_wide(weights, first_moment, second_moment, placement, block_counts, tokens, hidden_grad):
     expert_count = lax.axis_size("expert")
     dp_count = lax.axis_size("dp")
     block_total, span_rows, col_total = weights.shape
@@ -78,6 +82,327 @@
     return (updated[None], one_here[None], two_here[None])
 
 
+MESH = pl.DeviceIdType.MESH
+VMEM_BYTES = 60 * 1024 * 1024
+
+
+def plane_size(expert_count):
+    size = 1
+    while 4 * size * size <= expert_count:
+        size *= 2
+    return size
+
+
+def remote(source, target, send_sem, recv_sem, axis, index):
+    return pltpu.make_async_remote_copy(
+        src_ref=source, dst_ref=target, send_sem=send_sem, recv_sem=recv_sem,
+        device_id={axis: index}, device_id_type=MESH,
+    )
+
+
+def greet(level, levels, near, me, with_dp):
+    barrier = pltpu.get_barrier_semaphore()
+
+    def signal(axis, index):
+        pl.semaphore_signal(barrier, inc=1, device_id={axis: index}, device_id_type=MESH)
+
+    for step in range(1, near):
+        signal("expert", me - me % near + ((me % near) ^ step))
+    if with_dp:
+        signal("dp", 1 - lax.axis_index("dp"))
+    pl.when(level > 0)(lambda: signal("expert", me - near))
+    pl.when(level < levels - 1)(lambda: signal("expert", me + near))
+    count = near - 1 + int(with_dp)
+    pl.semaphore_wait(
+        barrier, count + (level > 0).astype(jnp.int32) + (level < levels - 1).astype(jnp.int32)
+    )
+
+
+def gather_kernel(channels, levels, near, with_tokens, *refs):
+    slots = channels * (levels - 1)
+    fixed = 5 if with_tokens else 3
+    from_below, from_above = refs[fixed:fixed + slots], refs[fixed + slots:fixed + 2 * slots]
+    refs = refs[:fixed] + refs[fixed + 2 * slots:]
+
+    def slot(channel, hop):
+        return channel * (levels - 1) + hop
+
+    if with_tokens:
+        (place, slab, tokens, out, inputs, chosen,
+         up_send, up_recv, down_send, down_recv, near_send, near_recv, dp_send, dp_recv, own_sem) = refs
+    else:
+        (place, slab, out, chosen,
+         up_send, up_recv, down_send, down_recv, near_send, near_recv) = refs
+    me = lax.axis_index("expert")
+    level, spot = me // near, me % near
+    greet(level, levels, near, me, with_tokens)
+
+    def up(channel, hop):
+        source = slab.at[channel] if hop == 0 else from_below[slot(channel, hop - 1)]
+        return remote(source, from_below[slot(channel, hop)], up_send.at[channel, hop],
+                      up_recv.at[channel, hop], "expert", me + near)
+
+    def down(channel, hop):
+        source = slab.at[channel] if hop == 0 else from_above[slot(channel, hop - 1)]
+        return remote(source, from_above[slot(channel, hop)], down_send.at[channel, hop],
+                      down_recv.at[channel, hop], "expert", me - near)
+
+    def across(channel, origin, step):
+        return remote(chosen.at[channel, origin, step - 1], out.at[channel, origin, spot],
+                      near_send.at[channel, origin, step - 1], near_recv.at[channel, origin, step - 1],
+                      "expert", level * near + (spot ^ step))
+
+    def hand_on(channel, origin, held):
+        for step in range(1, near):
+            chosen[channel, origin, step - 1] = held[place[level * near + (spot ^ step)]]
+            across(channel, origin, step).start()
+        out[channel, origin, spot] = held[place[me]]
+
+    for channel in range(channels):
+        pl.when(level < levels - 1)(lambda c=channel: up(c, 0).start())
+        pl.when(level > 0)(lambda c=channel: down(c, 0).start())
+    if with_tokens:
+        core = lax.axis_index("dp")
+        width = inputs.shape[2]
+        other = 1 - core
+
+        def columns(index):
+            return tokens.at[:, pl.ds(pl.multiple_of(index * width, 128), width)]
+
+        swap = remote(columns(other), inputs.at[core], dp_send, dp_recv, "dp", other)
+        swap.start()
+        keep = pltpu.make_async_copy(columns(core), inputs.at[core], own_sem)
+        keep.start()
+    for channel in range(channels):
+        hand_on(channel, level, slab.at[channel])
+    for hop in range(levels - 1):
+        for channel in range(channels):
+
+            @pl.when(level > hop)
+            def _():
+                up(channel, hop).wait_recv()
+                if hop < levels - 2:
+                    pl.when(level < levels - 1)(lambda: up(channel, hop + 1).start())
+                hand_on(channel, level - hop - 1, from_below[slot(channel, hop)])
+
+            @pl.when(level < levels - 1 - hop)
+            def _():
+                down(channel, hop).wait_recv()
+                if hop < levels - 2:
+                    pl.when(level > 0)(lambda: down(channel, hop + 1).start())
+                hand_on(channel, level + hop + 1, from_above[slot(channel, hop)])
+
+    for channel in range(channels):
+        for hop in range(levels - 1):
+            pl.when((level < levels - 1) & (level >= hop))(lambda c=channel, h=hop: up(c, h).wait_send())
+            pl.when((level > 0) & (level < levels - hop))(lambda c=channel, h=hop: down(c, h).wait_send())
+        for origin in range(levels):
+            for step in range(1, near):
+                across(channel, origin, step).wait()
+    if with_tokens:
+        swap.wait()
+        keep.wait()
+
+
+def reduce_kernel(levels, near, place, term, out, arrived, below, above, to_up, to_down,
+                  up_send, up_recv, down_send, down_recv, near_send, near_recv):
+    me = lax.axis_index("expert")
+    level, spot = me // near, me % near
+    blocks, rows, cols = out.shape
+    greet(level, levels, near, me, False)
+
+    def across(goal, step):
+        return remote(term.at[goal, spot ^ step], arrived.at[goal, step - 1],
+                      near_send.at[goal, step - 1], near_recv.at[goal, step - 1],
+                      "expert", level * near + (spot ^ step))
+
+    def up(left):
+        return remote(to_up.at[left - 1], below.at[left - 1], up_send.at[left - 1],
+                      up_recv.at[left - 1], "expert", me + near)
+
+    def down(left):
+        return remote(to_down.at[left - 1], above.at[left - 1], down_send.at[left - 1],
+                      down_recv.at[left - 1], "expert", me - near)
+
+    def start_near(goal):
+        for step in range(1, near):
+            across(goal, step).start()
+
+    def sums(goal, target, extra):
+        for step in range(1, near):
+            across(goal, step).wait_recv()
+        owners = [place[level * near + (spot ^ step)] for step in range(near)]
+
+        @pl.loop(0, rows // 16)
+        def _(tile):
+            here = pl.ds(pl.multiple_of(tile * 16, 16), 16)
+            terms = [term[goal, spot, here, :].astype(jnp.float32)]
+            terms += [arrived[goal, step - 1, here, :].astype(jnp.float32) for step in range(1, near)]
+            for block in range(blocks):
+                total = None
+                for owner, value in zip(owners, terms):
+                    part = jnp.where(owner == block, 1.0, 0.0) * value
+                    total = part if total is None else total + part
+                for ref in extra:
+                    total = total + ref[block, here, :].astype(jnp.float32)
+                target[block, here, :] = total.astype(target.dtype)
+
+    for left in range(levels - 1, 0, -1):
+        pl.when(level + left < levels)(lambda n=left: start_near(level + n))
+        pl.when(level >= left)(lambda n=left: start_near(level - n))
+    start_near(level)
+    for left in range(levels - 1, 0, -1):
+
+        @pl.when(level + left < levels)
+        def _():
+            if left < levels - 1:
+                @pl.when(level > 0)
+                def _():
+                    up(left + 1).wait_recv()
+                    sums(level + left, to_up.at[left - 1], [below.at[left]])
+
+            @pl.when(level == 0)
+            def _():
+                sums(level + left, to_up.at[left - 1], [])
+
+            up(left).start()
+
+        @pl.when(level >= left)
+        def _():
+            if left < levels - 1:
+                @pl.when(level < levels - 1)
+                def _():
+                    down(left + 1).wait_recv()
+                    sums(level - left, to_down.at[left - 1], [above.at[left]])
+
+            @pl.when(level == levels - 1)
+            def _():
+                sums(level - left, to_down.at[left - 1], [])
+
+            down(left).start()
+
+    sums(level, out, [])
+
+    def add(ref):
+        @pl.loop(0, rows // 16)
+        def _(tile):
+            here = pl.ds(pl.multiple_of(tile * 16, 16), 16)
+            for block in range(blocks):
+                out[block, here, :] += ref[block, here, :].astype(jnp.float32)
+
+    @pl.when(level > 0)
+    def _():
+        up(1).wait_recv()
+        add(below.at[0])
+
+    @pl.when(level < levels - 1)
+    def _():
+        down(1).wait_recv()
+        add(above.at[0])
+
+    for left in range(1, levels):
+        pl.when(level + left < levels)(lambda n=left: up(n).wait_send())
+        pl.when(level >= left)(lambda n=left: down(n).wait_send())
+    for goal in range(levels):
+        for step in range(1, near):
+            across(goal, step).wait_send()
+
+
+def in_vmem():
+    return pl.BlockSpec(memory_space=pltpu.VMEM)
+
+
+def in_smem():
+    return pl.BlockSpec(memory_space=pltpu.SMEM)
+
+
+def call_gather(placement, slab, levels, near, collective_id, tokens=None):
+    channels, blocks, rows, cols = slab.shape
+    kind = slab.dtype
+    out_shape = [jax.ShapeDtypeStruct((channels, levels, near, rows, cols), kind)]
+    in_specs = [in_smem(), in_vmem()]
+    operands = [placement, slab]
+    out_specs = [in_vmem()]
+    dma = pltpu.SemaphoreType.DMA
+    scratch = [pltpu.VMEM((blocks, rows, cols), kind)] * (2 * channels * (levels - 1))
+    scratch += [pltpu.VMEM((channels, levels, near - 1, rows, cols), kind)]
+    scratch += [dma((channels, levels - 1))] * 4 + [dma((channels, levels, near - 1))] * 2
+    if tokens is not None:
+        count, width = tokens.shape
+        out_shape.append(jax.ShapeDtypeStruct((2, count, width // 2), tokens.dtype))
+        in_specs.append(in_vmem())
+        operands.append(tokens)
+        out_specs.append(in_vmem())
+        scratch += [dma, dma, dma]
+    return pl.pallas_call(
+        functools.partial(gather_kernel, channels, levels, near, tokens is not None),
+        out_shape=out_shape, in_specs=in_specs, out_specs=out_specs, scratch_shapes=scratch,
+        compiler_params=pltpu.CompilerParams(
+            collective_id=collective_id, has_side_effects=True, vmem_limit_bytes=VMEM_BYTES
+        ),
+    )(*operands)
+
+
+def call_reduce(placement, term, blocks, collective_id):
+    levels, near, rows, cols = term.shape
+    kind = term.dtype
+    dma = pltpu.SemaphoreType.DMA
+    return pl.pallas_call(
+        functools.partial(reduce_kernel, levels, near),
+        out_shape=jax.ShapeDtypeStruct((blocks, rows, cols), jnp.float32),
+        in_specs=[in_smem(), in_vmem()], out_specs=in_vmem(),
+        scratch_shapes=[pltpu.VMEM((levels, near - 1, rows, cols), kind)]
+        + [pltpu.VMEM((levels - 1, blocks, rows, cols), kind)] * 4
+        + [dma((levels - 1,))] * 4 + [dma((levels, near - 1))] * 2,
+        compiler_params=pltpu.CompilerParams(
+            collective_id=collective_id, has_side_effects=True, vmem_limit_bytes=VMEM_BYTES
+        ),
+    )(placement, term)
+
+
+def on_device(weights, first_moment, second_moment, placement, block_counts, tokens, hidden_grad):
+    expert_count = lax.axis_size("expert")
+    dp_count = lax.axis_size("dp")
+    block_total, span_rows, col_total = weights.shape
+    row_total, model = tokens.shape[2:]
+    near = plane_size(expert_count)
+    levels = expert_count // near
+    fits = dp_count == 2 and near > 1 and levels > 1 and levels * near == expert_count
+    if not fits or span_rows % 16 or model % 256 or col_total % 128 or row_total % 16:
+        return on_device_wide(
+            weights, first_moment, second_moment, placement, block_counts, tokens, hidden_grad
+        )
+    part_rows = expert_count * span_rows
+    core = lax.axis_index("dp")
+    swap = [(0, 1), (1, 0)]
+    live_mask = (jnp.arange(row_total) < BLOCK * block_counts[0, 0])[:, None]
+
+    own_rows, inputs = call_gather(placement, weights[None], levels, near, 0, tokens[0, 0])
+    own_rows = own_rows.reshape(part_rows, col_total)
+    inputs = inputs.reshape(2 * row_total, model // 2)
+    mine = lax.dynamic_slice_in_dim(inputs, core * row_total, row_total)
+    others = lax.dynamic_slice_in_dim(inputs, (1 - core) * row_total, row_total)
+    away = jnp.dot(others, own_rows, preferred_element_type=jnp.float32)
+    away = lax.ppermute(away, "dp", swap)
+    projected = jnp.dot(mine, own_rows, preferred_element_type=jnp.float32) + away
+    grad_here = silu_grads(projected, hidden_grad[0, 0], live_mask)
+    grad_away = lax.ppermute(grad_here, "dp", swap)
+    down = (((0,), (0,)), ((), ()))
+    ordered = jnp.where(core == 0, jnp.stack([grad_here, grad_away]), jnp.stack([grad_away, grad_here]))
+    term = lax.dot_general(
+        inputs, ordered.reshape(2 * row_total, col_total), down, preferred_element_type=jnp.float32
+    ).astype(jnp.bfloat16)
+    block_grad = call_reduce(
+        placement, term.reshape(levels, near, span_rows, col_total), block_total, 1
+    )
+    moment_one, moment_two = moments(first_moment, second_moment, block_grad)
+    both = jnp.stack([moment_one.astype(jnp.bfloat16), moment_two.astype(jnp.bfloat16)])
+    (here,) = call_gather(placement, both, levels, near, 2)
+    here = here.reshape(2, part_rows, col_total).astype(jnp.float32)
+    updated = new_params(own_rows, here[0], here[1])
+    return (updated[None], here[0][None], here[1][None])
+
+
 def solution(mesh):
     in_specs = (
         P(None, ("dp", "expert"), None),

time: 298 us -> 181 us (0.61)
  Pallas kernels: 0 us -> 159 us
  blocking collectives: 146 us -> 0 us
  waiting for transfers between devices: 46.6 us -> 2.64 us
  local copies, waits for them, and re-layouts: 44.2 us -> 3.25 us
  other arithmetic: 26.4 us -> 6.84 us
  between operations: 14.8 us -> 1.43 us
  starting transfers between devices: 12.2 us -> 0.27 us
    pallas_call x0 -> x3, Pallas kernels: none -> 159 us  [the longest x2 116 us: call_gather(): pl.pallas_call(functools.partial(gather_kernel, channels, levels, near, t...]
    all_to_all x3 -> x0, blocking collectives: 144 us -> none  [exchange(): return lax.all_to_all(x, axis, split_axis=0, concat_axis=0, tiled=True)]
    all_to_all x2 -> x0, waiting for transfers between devices: 35 us -> none  [the longest x1 35 us: exchange(): return lax.all_to_all(x, axis, split_axis=0, concat_axis=0, tiled=True)]
    unnamed x19 -> x12, local copies, waits for them, and re-layouts: 24.1 us -> 0.03 us
    all_to_all x1 -> x0, other arithmetic: 13.6 us -> none  [exchange(): return lax.all_to_all(x, axis, split_axis=0, concat_axis=0, tiled=True)]
    all_to_all x2 -> x0, starting transfers between devices: 12.2 us -> none  [the longest x1 8.34 us: exchange(): return lax.all_to_all(x, axis, split_axis=0, concat_axis=0, tiled=True)]
    reduce_scatter x1 -> x0, waiting for transfers between devices: 11.6 us -> none  [on_device(): projected = lax.psum_scatter(partial, 'dp', scatter_dimension=0, tiled=True)]
    all_to_all x3 -> x0, local copies, waits for them, and re-layouts: 10.6 us -> none  [the longest x2 6.72 us: exchange(): return lax.all_to_all(x, axis, split_axis=0, concat_axis=0, tiled=True)]
  transfers between devices with their start and end apart: 3 -> 2, of which waited for: 2 -> 2; matrix products, arithmetic and copies ran while one was open for 3% -> 0% of each run, Pallas kernels for 0% -> 0%
where the time goes in v2:
time: 181 us
  Pallas kernels  159 us (88%)
  matrix products  7.36 us (4%)
  other arithmetic  6.84 us (4%)
  local copies, waits for them, and re-layouts  3.25 us (2%)
  waiting for transfers between devices  2.64 us (1%)
    pallas_call x2, Pallas kernels, call_gather(): pl.pallas_call(functools.partial(gather_kernel, channels, levels, near, t...  116 us
    pallas_call x1, Pallas kernels, call_reduce(): pl.pallas_call(functools.partial(reduce_kernel, levels, near), out_shape=...  43.1 us
    convert_element_type x1, other arithmetic, new_params(): return (params_full - learning_rate * step_size).astype(jnp.bfloat16)  3.81 us
  transfers between devices with their start and end apart: 2, of which 2 were waited for; matrix products, arithmetic and copies ran while one was open for 0% of the time, Pallas kernels for 0%

profile of v2, /device:TPU:0, one launch (start us, length us, event | category | flops | bytes accessed | tf_op | source)
XLA Modules:
  0.0 180.8 jit_solution(10754417720124235387)
XLA Ops:
  0.6 47.4 %shard_map.94 = (bf16[1,4,4,112,512]{4,3,2,1,0:T(8,128)(2,1)}, bf16[2,256,1792]{2,1,0:T(8,128)(2,1)}) custom-call(s32[16]{0:T(128)} %refs_0_.3, bf16[1,4,112,512]{3,2,1,0:T(8,128)(2,1)} %bitcast.39, bf16[256,3584]{1,0:T(8,128)(2,1)} %bitcast.33), custom_call_target="tpu_custom_call" | custom-call | tf_op jit(solution)/shard_map/pallas_call | solution.py:337
  48.1 0.0 copy-start.5
  48.1 0.0 copy-start.3
  48.1 2.6 %fusion.5 = f32[256,512]{1,0:T(8,128)S(1)} fusion(bf16[1792,512]{1,0:T(8,128)(2,1)} %bitcast.29, bf16[512,1792]{1,0:T(8,128)(2,1)} %bitcast.35, s32[]{:T(128)S(6)} %select_n.21), kind=kOutput, calls=%fused_computation.12 | convolution fusion | flops 469762048 | bytes 3276804 | tf_op jit(solution)/shard_map/dot_general | solution.py:385
  50.7 0.1 collective-permute-start
  51.4 1.2 collective-permute-done
  52.6 2.4 %convolution_add_fusion = f32[256,512]{1,0:T(8,128)S(1)} fusion(f32[256,512]{1,0:T(8,128)S(1)} %collective-permute-done, bf16[1792,512]{1,0:T(8,128)(2,1)} %bitcast.30, bf16[512,1792]{1,0:T(8,128)(2,1)} %bitcast.36, s32[]{:T(128)S(6)} %select_n.20), kind=kOutput, calls=%fused_computation.7 | convolution fusion | flops 469893120 | bytes 3801092 | tf_op jit(solution)/shard_map/dot_general | solution.py:387
  55.1 0.0 copy-done.5
  55.1 0.2 fusion.22
  55.3 0.2 collective-permute-start.1
  55.5 1.4 collective-permute-done.1
  56.9 0.0 copy-done.3
  56.9 0.0 copy-start.4
  56.9 2.4 %bitcast_convert_fusion = bf16[1792,512]{1,0:T(8,128)(2,1)} fusion(bf16[2,256,1792]{2,1,0:T(8,128)(2,1)S(1)} %copy-done.3, bf16[1,256,512]{2,1,0:T(8,128)(2,1)S(1)} %bitcast.40, bf16[1,256,256]{2,1,0:T(8,128)(2,1)S(1)} %bitcast.38, bf16[1,256,256]{2,1,0:T(8,128)(2,1)S(1)} %bitcast.37, pred[]{:T(512)S(6)} %eq.3), kind=kOutput, calls=%fused_computation.5 | convolution fusion | flops 943849472 | bytes 4194305 | tf_op jit(solution)/shard_map/dot_general | solution.py:392
  59.3 43.1 %shard_map.95 = f32[4,112,512]{2,1,0:T(8,128)} custom-call(s32[16]{0:T(128)} %refs_0_.3, bf16[4,4,112,512]{3,2,1,0:T(8,128)(2,1)} %bitcast.34), custom_call_target="tpu_custom_call" | custom-call | tf_op jit(solution)/shard_map/pallas_call | solution.py:350
  102.4 0.0 copy-done.4
  102.4 1.8 %fusion.18 = (bf16[1,4,112,512]{3,2,1,0:T(8,128)(2,1)S(1)}, bf16[1,4,112,512]{3,2,1,0:T(8,128)(2,1)S(1)}) fusion(f32[4,112,512]{2,1,0:T(8,128)} %shard_map.95, f32[4,112,512]{2,1,0:T(8,128)S(1)} %copy-done.4, f32[4,112,512]{2,1,0:T(8,128)} %param.9), kind=kLoop, calls=%fused_computation.26 | loop fusion | flops 2064384 | bytes 3670016 | tf_op jit(solution)/shard_map/stack | solution.py:399
  104.2 1.0 pad_maximum_fusion.refs_1_
  105.2 68.4 %shard_map.96 = bf16[2,4,4,112,512]{4,3,2,1,0:T(8,128)(2,1)} custom-call(s32[16]{0:T(128)} %refs_0_.3, bf16[2,4,112,512]{3,2,1,0:T(8,128)(2,1)} %pad_maximum_fusion.refs_1_), custom_call_target="tpu_custom_call" | custom-call | tf_op jit(solution)/shard_map/pallas_call | solution.py:337
  173.7 0.0 copy-start
  173.7 3.2 %fusion.29 = (f32[1,4,4,112,512]{4,3,2,1,0:T(8,128)S(1)}, f32[1,4,4,112,512]{4,3,2,1,0:T(8,128)S(1)}) fusion(bf16[2,4,4,112,512]{4,3,2,1,0:T(8,128)(2,1)} %shard_map.96), kind=kLoop, calls=%fused_computation.42 | loop fusion | bytes 14680064 | tf_op jit(solution)/shard_map/slice | solution.py:402
  176.9 0.0 copy-start.1
  176.9 0.0 copy-start.2
  176.9 0.0 copy-done
  176.9 3.8 %fusion.2 = bf16[1,1792,512]{2,1,0:T(8,128)(2,1)} fusion(bf16[1,4,4,112,512]{4,3,2,1,0:T(8,128)(2,1)S(1)} %copy-done, f32[1,4,4,112,512]{4,3,2,1,0:T(8,128)S(1)} %get-tuple-element.7, f32[1,4,4,112,512]{4,3,2,1,0:T(8,128)S(1)} %get-tuple-element.8), kind=kLoop, calls=%fused_computation.4 | loop fusion | flops 9175040 | bytes 11010048 | tf_op jit(solution)/shard_map/convert_element_type | solution.py:46
  180.8 0.0 copy-done.1
  180.8 0.0 copy-done.2
  (2 shorter events, 0.0 us)
Async XLA Ops:
  48.1 7.0 %copy-start.5 = (bf16[1,1,256,256]{3,2,1,0:T(8,128)(2,1)S(1)}, bf16[1,1,256,256]{3,2,1,0:T(8,128)(2,1)}, u32[]{:S(2)}) copy-start(bf16[1,1,256,256]{3,2,1,0:T(8,128)(2,1)} %param.13) | copy-start | bytes 393220
  48.1 8.8 %copy-start.3 = (bf16[2,256,1792]{2,1,0:T(8,128)(2,1)S(1)}, bf16[2,256,1792]{2,1,0:T(8,128)(2,1)}, u32[]{:S(2)}) copy-start(bf16[2,256,1792]{2,1,0:T(8,128)(2,1)} %get-tuple-element.6) | copy-start | bytes 5505028
  50.7 2.0 %collective-permute-start = (f32[256,512]{1,0:T(8,128)S(1)}, f32[256,512]{1,0:T(8,128)S(1)}, u32[]{:S(2)}, u32[]{:S(2)}) collective-permute-start(f32[256,512]{1,0:T(8,128)S(1)} %fusion.5), channel_id=1, source_target_pairs={{0,16},{16,0},{1,17},{17,1},{2,18},{18,2},{3,19},{19,3},{4,20},{20... | collective-permute-start | bytes 1572872 | tf_op jit(solution)/shard_map/ppermute | solution.py:386
  55.3 1.6 collective-permute-start.1
  56.9 45.5 %copy-start.4 = (f32[4,112,512]{2,1,0:T(8,128)S(1)}, f32[4,112,512]{2,1,0:T(8,128)}, u32[]{:S(2)}) copy-start(f32[4,112,512]{2,1,0:T(8,128)} %param.8) | copy-start | bytes 2752516
  173.7 3.3 %copy-start = (bf16[1,4,4,112,512]{4,3,2,1,0:T(8,128)(2,1)S(1)}, bf16[1,4,4,112,512]{4,3,2,1,0:T(8,128)(2,1)}, u32[]{:S(2)}) copy-start(bf16[1,4,4,112,512]{4,3,2,1,0:T(8,128)(2,1)} %get-tuple-element.5) | copy-start | bytes 5505028
  176.9 3.9 %copy-start.1 = (f32[1,4,4,112,512]{4,3,2,1,0:T(8,128)}, f32[1,4,4,112,512]{4,3,2,1,0:T(8,128)S(1)}, u32[]{:S(2)}) copy-start(f32[1,4,4,112,512]{4,3,2,1,0:T(8,128)S(1)} %get-tuple-element.7) | copy-start | bytes 11010052
  176.9 3.8 %copy-start.2 = (f32[1,4,4,112,512]{4,3,2,1,0:T(8,128)}, f32[1,4,4,112,512]{4,3,2,1,0:T(8,128)S(1)}, u32[]{:S(2)}) copy-start(f32[1,4,4,112,512]{4,3,2,1,0:T(8,128)S(1)} %get-tuple-element.8) | copy-start | bytes 11010052

commit v3 on v2

--- a/solution.py
+++ b/solution.py
@@ -84,6 +84,7 @@
 
 MESH = pl.DeviceIdType.MESH
 VMEM_BYTES = 60 * 1024 * 1024
+PIECES = 2
 
 
 def plane_size(expert_count):
@@ -204,40 +205,53 @@
         keep.wait()
 
 
-def reduce_kernel(levels, near, place, term, out, arrived, below, above, to_up, to_down,
-                  up_send, up_recv, down_send, down_recv, near_send, near_recv):
+def update_kernel(levels, near, cuts, *refs):
+    place, term, first, second, out = refs[:5]
+    chunks, hops = len(cuts), levels - 1
+    at = [5]
+
+    def take(count):
+        at[0] += count
+        return refs[at[0] - count:at[0]]
+
+    arrived, below, above, to_up, to_down, slabs, picked = (take(chunks) for _ in range(7))
+    from_below, from_above = take(chunks * hops), take(chunks * hops)
+    (sum_up_send, sum_up_recv, sum_down_send, sum_down_recv, sum_near_send, sum_near_recv,
+     up_send, up_recv, down_send, down_recv, near_send, near_recv) = refs[at[0]:]
     me = lax.axis_index("expert")
     level, spot = me // near, me % near
-    blocks, rows, cols = out.shape
+    blocks, _, cols = first.shape
+    starts = [sum(cuts[:chunk]) for chunk in range(chunks)]
     greet(level, levels, near, me, False)
 
-    def across(goal, step):
-        return remote(term.at[goal, spot ^ step], arrived.at[goal, step - 1],
-                      near_send.at[goal, step - 1], near_recv.at[goal, step - 1],
+    def sum_across(chunk, goal, step):
+        rows = pl.ds(starts[chunk], cuts[chunk])
+        return remote(term.at[goal, spot ^ step, rows], arrived[chunk].at[goal, step - 1],
+                      sum_near_send.at[chunk, goal, step - 1], sum_near_recv.at[chunk, goal, step - 1],
                       "expert", level * near + (spot ^ step))
 
-    def up(left):
-        return remote(to_up.at[left - 1], below.at[left - 1], up_send.at[left - 1],
-                      up_recv.at[left - 1], "expert", me + near)
-
-    def down(left):
-        return remote(to_down.at[left - 1], above.at[left - 1], down_send.at[left - 1],
-                      down_recv.at[left - 1], "expert", me - near)
-
-    def start_near(goal):
+    def sum_up(chunk, left):
+        return remote(to_up[chunk].at[left - 1], below[chunk].at[left - 1], sum_up_send.at[chunk, left - 1],
+                      sum_up_recv.at[chunk, left - 1], "expert", me + near)
+
+    def sum_down(chunk, left):
+        return remote(to_down[chunk].at[left - 1], above[chunk].at[left - 1],
+                      sum_down_send.at[chunk, left - 1], sum_down_recv.at[chunk, left - 1],
+                      "expert", me - near)
+
+    def sum_start(chunk, goal):
         for step in range(1, near):
-            across(goal, step).start()
-
-    def sums(goal, target, extra):
-        for step in range(1, near):
-            across(goal, step).wait_recv()
+            sum_across(chunk, goal, step).start()
+
+    def sums(chunk, goal, extra, emit):
         owners = [place[level * near + (spot ^ step)] for step in range(near)]
 
-        @pl.loop(0, rows // 16)
+        @pl.loop(0, cuts[chunk] // 16)
         def _(tile):
             here = pl.ds(pl.multiple_of(tile * 16, 16), 16)
-            terms = [term[goal, spot, here, :].astype(jnp.float32)]
-            terms += [arrived[goal, step - 1, here, :].astype(jnp.float32) for step in range(1, near)]
+            there = pl.ds(pl.multiple_of(starts[chunk] + tile * 16, 16), 16)
+            terms = [term[goal, spot, there, :].astype(jnp.float32)]
+            terms += [arrived[chunk][goal, step - 1, here, :].astype(jnp.float32) for step in range(1, near)]
             for block in range(blocks):
                 total = None
                 for owner, value in zip(owners, terms):
@@ -245,67 +259,132 @@
                     total = part if total is None else total + part
                 for ref in extra:
                     total = total + ref[block, here, :].astype(jnp.float32)
+                emit(block, here, there, total)
+
+    def await_near(chunk, goal):
+        for step in range(1, near):
+            sum_across(chunk, goal, step).wait_recv()
+
+    def pass_on(chunk, left):
+        def emit_to(target):
+            def emit(block, here, there, total):
                 target[block, here, :] = total.astype(target.dtype)
-
-    for left in range(levels - 1, 0, -1):
-        pl.when(level + left < levels)(lambda n=left: start_near(level + n))
-        pl.when(level >= left)(lambda n=left: start_near(level - n))
-    start_near(level)
-    for left in range(levels - 1, 0, -1):
+            return emit
 
         @pl.when(level + left < levels)
         def _():
-            if left < levels - 1:
+            goal, target = level + left, to_up[chunk].at[left - 1]
+            await_near(chunk, goal)
+            if left < hops:
                 @pl.when(level > 0)
                 def _():
-                    up(left + 1).wait_recv()
-                    sums(level + left, to_up.at[left - 1], [below.at[left]])
-
-            @pl.when(level == 0)
-            def _():
-                sums(level + left, to_up.at[left - 1], [])
-
-            up(left).start()
+                    sum_up(chunk, left + 1).wait_recv()
+                    sums(chunk, goal, [below[chunk].at[left]], emit_to(target))
+            pl.when(level == 0)(lambda: sums(chunk, goal, [], emit_to(target)))
+            sum_up(chunk, left).start()
 
         @pl.when(level >= left)
         def _():
-            if left < levels - 1:
+            goal, target = level - left, to_down[chunk].at[left - 1]
+            await_near(chunk, goal)
+            if left < hops:
                 @pl.when(level < levels - 1)
                 def _():
-                    down(left + 1).wait_recv()
-                    sums(level - left, to_down.at[left - 1], [above.at[left]])
-
-            @pl.when(level == levels - 1)
-            def _():
-                sums(level - left, to_down.at[left - 1], [])
-
-            down(left).start()
-
-    sums(level, out, [])
-
-    def add(ref):
-        @pl.loop(0, rows // 16)
-        def _(tile):
-            here = pl.ds(pl.multiple_of(tile * 16, 16), 16)
-            for block in range(blocks):
-                out[block, here, :] += ref[block, here, :].astype(jnp.float32)
-
-    @pl.when(level > 0)
-    def _():
-        up(1).wait_recv()
-        add(below.at[0])
-
-    @pl.when(level < levels - 1)
-    def _():
-        down(1).wait_recv()
-        add(above.at[0])
-
-    for left in range(1, levels):
-        pl.when(level + left < levels)(lambda n=left: up(n).wait_send())
-        pl.when(level >= left)(lambda n=left: down(n).wait_send())
-    for goal in range(levels):
+                    sum_down(chunk, left + 1).wait_recv()
+                    sums(chunk, goal, [above[chunk].at[left]], emit_to(target))
+            pl.when(level == levels - 1)(lambda: sums(chunk, goal, [], emit_to(target)))
+            sum_down(chunk, left).start()
+
+    def up(chunk, hop):
+        source = slabs[chunk] if hop == 0 else from_below[chunk * hops + hop - 1]
+        return remote(source, from_below[chunk * hops + hop], up_send.at[chunk, hop],
+                      up_recv.at[chunk, hop], "expert", me + near)
+
+    def down(chunk, hop):
+        source = slabs[chunk] if hop == 0 else from_above[chunk * hops + hop - 1]
+        return remote(source, from_above[chunk * hops + hop], down_send.at[chunk, hop],
+                      down_recv.at[chunk, hop], "expert", me - near)
+
+    def across(chunk, origin, step):
+        rows = pl.ds(starts[chunk], cuts[chunk])
+        return remote(picked[chunk].at[origin, step - 1], out.at[:, origin, spot, rows],
+                      near_send.at[chunk, origin, step - 1], near_recv.at[chunk, origin, step - 1],
+                      "expert", level * near + (spot ^ step))
+
+    def hand_on(chunk, origin, held):
         for step in range(1, near):
-            across(goal, step).wait_send()
+            picked[chunk][origin, step - 1] = held[place[level * near + (spot ^ step)]]
+            across(chunk, origin, step).start()
+        out[:, origin, spot, pl.ds(starts[chunk], cuts[chunk]), :] = held[place[me]]
+
+    def settle(chunk):
+        def emit(block, here, there, total):
+            slabs[chunk][block, 0, here, :] = (
+                beta_first * first[block, there, :] + (1.0 - beta_first) * total
+            ).astype(out.dtype)
+            slabs[chunk][block, 1, here, :] = (
+                beta_second * second[block, there, :] + (1.0 - beta_second) * total * total
+            ).astype(out.dtype)
+
+        await_near(chunk, level)
+        pl.when(level > 0)(lambda: sum_up(chunk, 1).wait_recv())
+        pl.when(level < levels - 1)(lambda: sum_down(chunk, 1).wait_recv())
+        under, over = below[chunk].at[0], above[chunk].at[0]
+        pl.when(level == 0)(lambda: sums(chunk, level, [over], emit))
+        pl.when(level == levels - 1)(lambda: sums(chunk, level, [under], emit))
+        pl.when((level > 0) & (level < levels - 1))(lambda: sums(chunk, level, [under, over], emit))
+        pl.when(level < levels - 1)(lambda: up(chunk, 0).start())
+        pl.when(level > 0)(lambda: down(chunk, 0).start())
+        hand_on(chunk, level, slabs[chunk])
+
+    def forward(chunk, hop):
+        @pl.when(level > hop)
+        def _():
+            up(chunk, hop).wait_recv()
+            if hop < hops - 1:
+                pl.when(level < levels - 1)(lambda: up(chunk, hop + 1).start())
+            hand_on(chunk, level - hop - 1, from_below[chunk * hops + hop])
+
+        @pl.when(level < levels - 1 - hop)
+        def _():
+            down(chunk, hop).wait_recv()
+            if hop < hops - 1:
+                pl.when(level > 0)(lambda: down(chunk, hop + 1).start())
+            hand_on(chunk, level + hop + 1, from_above[chunk * hops + hop])
+
+    for chunk in range(chunks):
+        for left in range(hops, 0, -1):
+            pl.when(level + left < levels)(lambda c=chunk, n=left: sum_start(c, level + n))
+            pl.when(level >= left)(lambda c=chunk, n=left: sum_start(c, level - n))
+        sum_start(chunk, level)
+
+    def stages(chunk):
+        return [functools.partial(pass_on, chunk, left) for left in range(hops, 0, -1)] + [
+            functools.partial(settle, chunk)
+        ]
+
+    for stage in stages(0):
+        stage()
+    for chunk in range(chunks):
+        coming = stages(chunk + 1) if chunk + 1 < chunks else []
+        if coming:
+            coming[0]()
+        for hop in range(hops):
+            if coming:
+                coming[hop + 1]()
+            forward(chunk, hop)
+
+    for chunk in range(chunks):
+        for left in range(1, levels):
+            pl.when(level + left < levels)(lambda c=chunk, n=left: sum_up(c, n).wait_send())
+            pl.when(level >= left)(lambda c=chunk, n=left: sum_down(c, n).wait_send())
+        for hop in range(hops):
+            pl.when((level < levels - 1) & (level >= hop))(lambda c=chunk, h=hop: up(c, h).wait_send())
+            pl.when((level > 0) & (level < levels - hop))(lambda c=chunk, h=hop: down(c, h).wait_send())
+        for goal in range(levels):
+            for step in range(1, near):
+                sum_across(chunk, goal, step).wait_send()
+                across(chunk, goal, step).wait()
 
 
 def in_vmem():
@@ -343,21 +422,38 @@
     )(*operands)
 
 
-def call_reduce(placement, term, blocks, collective_id):
+def call_update(placement, term, first, second, pieces, collective_id):
     levels, near, rows, cols = term.shape
+    blocks = first.shape[0]
     kind = term.dtype
+    tiles = rows // 16
+    pieces = min(pieces, tiles)
+    cuts = [16 * ((piece + 1) * tiles // pieces - piece * tiles // pieces) for piece in range(pieces)]
+    hops = levels - 1
     dma = pltpu.SemaphoreType.DMA
+
+    def each(make):
+        return [pltpu.VMEM(make(cut), kind) for cut in cuts]
+
+    scratch = each(lambda cut: (levels, near - 1, cut, cols))
+    for _ in range(4):
+        scratch += each(lambda cut: (hops, blocks, cut, cols))
+    scratch += each(lambda cut: (blocks, 2, cut, cols))
+    scratch += each(lambda cut: (levels, near - 1, 2, cut, cols))
+    for _ in range(2):
+        for cut in cuts:
+            scratch += [pltpu.VMEM((blocks, 2, cut, cols), kind)] * hops
+    scratch += [dma((pieces, hops))] * 4 + [dma((pieces, levels, near - 1))] * 2
+    scratch += [dma((pieces, hops))] * 4 + [dma((pieces, levels, near - 1))] * 2
     return pl.pallas_call(
-        functools.partial(reduce_kernel, levels, near),
-        out_shape=jax.ShapeDtypeStruct((blocks, rows, cols), jnp.float32),
-        in_specs=[in_smem(), in_vmem()], out_specs=in_vmem(),
-        scratch_shapes=[pltpu.VMEM((levels, near - 1, rows, cols), kind)]
-        + [pltpu.VMEM((levels - 1, blocks, rows, cols), kind)] * 4
-        + [dma((levels - 1,))] * 4 + [dma((levels, near - 1))] * 2,
+        functools.partial(update_kernel, levels, near, cuts),
+        out_shape=jax.ShapeDtypeStruct((2, levels, near, rows, cols), kind),
+        in_specs=[in_smem(), in_vmem(), in_vmem(), in_vmem()], out_specs=in_vmem(),
+        scratch_shapes=scratch,
         compiler_params=pltpu.CompilerParams(
             collective_id=collective_id, has_side_effects=True, vmem_limit_bytes=VMEM_BYTES
         ),
-    )(placement, term)
+    )(placement, term, first, second)
 
 
 def on_device(weights, first_moment, second_moment, placement, block_counts, tokens, hidden_grad):
@@ -392,12 +488,9 @@
     term = lax.dot_general(
         inputs, ordered.reshape(2 * row_total, col_total), down, preferred_element_type=jnp.float32
     ).astype(jnp.bfloat16)
-    block_grad = call_reduce(
-        placement, term.reshape(levels, near, span_rows, col_total), block_total, 1
+    here = call_update(
+        placement, term.reshape(levels, near, span_rows, col_total), first_moment, second_moment, PIECES, 1
     )
-    moment_one, moment_two = moments(first_moment, second_moment, block_grad)
-    both = jnp.stack([moment_one.astype(jnp.bfloat16), moment_two.astype(jnp.bfloat16)])
-    (here,) = call_gather(placement, both, levels, near, 2)
     here = here.reshape(2, part_rows, col_total).astype(jnp.float32)
     updated = new_params(own_rows, here[0], here[1])
     return (updated[None], here[0][None], here[1][None])

time: 181 us -> 166 us (0.917)
  Pallas kernels: 159 us -> 147 us
  other arithmetic: 6.84 us -> 4.01 us
    pallas_call x2 -> x1, Pallas kernels: 116 us -> 47.4 us  [call_gather(): pl.pallas_call(functools.partial(gather_kernel, channels, levels, near, t...]
    pallas_call x1, Pallas kernels: 43.1 us -> 99.5 us  [call_update(): pl.pallas_call(functools.partial(update_kernel, levels, near, cuts), out_...]
    another operation x3 -> x1, other arithmetic: 3 us -> 0.17 us  [the longest x2 2.83 us: on_device(): jnp.stack([moment_one.astype(jnp.bfloat16), moment_two.astype(jnp.bfloat1...]
where the time goes in v3:
time: 166 us
  Pallas kernels  147 us (89%)
  matrix products  7.36 us (4%)
  other arithmetic  4.01 us (2%)
  local copies, waits for them, and re-layouts  3.24 us (2%)
  waiting for transfers between devices  2.64 us (2%)
    pallas_call x1, Pallas kernels, call_update(): pl.pallas_call(functools.partial(update_kernel, levels, near, cuts), out_...  99.5 us
    pallas_call x1, Pallas kernels, call_gather(): pl.pallas_call(functools.partial(gather_kernel, channels, levels, near, t...  47.4 us
    convert_element_type x1, other arithmetic, new_params(): return (params_full - learning_rate * step_size).astype(jnp.bfloat16)  3.81 us
  transfers between devices with their start and end apart: 2, of which 2 were waited for; matrix products, arithmetic and copies ran while one was open for 0% of the time, Pallas kernels for 0%

profile of v3, /device:TPU:0, one launch (start us, length us, event | category | flops | bytes accessed | tf_op | source)
XLA Modules:
  0.0 165.9 jit_solution(12099741921037645556)
XLA Ops:
  0.6 47.4 %shard_map.94 = (bf16[1,4,4,112,512]{4,3,2,1,0:T(8,128)(2,1)}, bf16[2,256,1792]{2,1,0:T(8,128)(2,1)}) custom-call(s32[16]{0:T(128)} %refs_0_.3, bf16[1,4,112,512]{3,2,1,0:T(8,128)(2,1)} %bitcast.35, bf16[256,3584]{1,0:T(8,128)(2,1)} %bitcast.29), custom_call_target="tpu_custom_call" | custom-call | tf_op jit(solution)/shard_map/pallas_call | solution.py:416
  48.1 0.0 copy-start.4
  48.1 0.0 copy-start.3
  48.1 2.6 %fusion.3 = f32[256,512]{1,0:T(8,128)S(1)} fusion(bf16[1792,512]{1,0:T(8,128)(2,1)} %bitcast.25, bf16[512,1792]{1,0:T(8,128)(2,1)} %bitcast.30, s32[]{:T(128)S(6)} %select_n.21), kind=kOutput, calls=%fused_computation.7 | convolution fusion | flops 469762048 | bytes 3276804 | tf_op jit(solution)/shard_map/dot_general | solution.py:481
  50.7 0.1 collective-permute-start
  51.4 1.2 collective-permute-done
  52.6 2.4 %convolution_add_fusion = f32[256,512]{1,0:T(8,128)S(1)} fusion(f32[256,512]{1,0:T(8,128)S(1)} %collective-permute-done, bf16[1792,512]{1,0:T(8,128)(2,1)} %bitcast.26, bf16[512,1792]{1,0:T(8,128)(2,1)} %bitcast.31, s32[]{:T(128)S(6)} %select_n.20), kind=kOutput, calls=%fused_computation.6 | convolution fusion | flops 469893120 | bytes 3801092 | tf_op jit(solution)/shard_map/dot_general | solution.py:483
  55.1 0.0 copy-done.4
  55.1 0.2 fusion.18
  55.3 0.2 collective-permute-start.1
  55.5 1.4 collective-permute-done.1
  56.9 0.0 copy-done.3
  56.9 2.4 %bitcast_convert_fusion = bf16[1792,512]{1,0:T(8,128)(2,1)} fusion(bf16[2,256,1792]{2,1,0:T(8,128)(2,1)S(1)} %copy-done.3, bf16[1,256,512]{2,1,0:T(8,128)(2,1)S(1)} %bitcast.36, bf16[1,256,256]{2,1,0:T(8,128)(2,1)S(1)} %bitcast.34, bf16[1,256,256]{2,1,0:T(8,128)(2,1)S(1)} %bitcast.33, pred[]{:T(512)S(6)} %eq.3), kind=kOutput, calls=%fused_computation.5 | convolution fusion | flops 943849472 | bytes 4194305 | tf_op jit(solution)/shard_map/dot_general | solution.py:488
  59.3 99.5 %shard_map.95 = bf16[2,4,4,112,512]{4,3,2,1,0:T(8,128)(2,1)} custom-call(s32[16]{0:T(128)} %refs_0_.3, bf16[4,4,112,512]{3,2,1,0:T(8,128)(2,1)} %bitcast.32, f32[4,112,512]{2,1,0:T(8,128)} %refs_2_.1, f32[4,112,512]{2,1,0:T(8,128)} %refs_3_.1), custom_call_target="tpu_custom_call" | custom-call | tf_op jit(solution)/shard_map/pallas_call | solution.py:448
  158.8 0.0 copy-start
  158.8 3.2 %fusion.25 = (f32[1,4,4,112,512]{4,3,2,1,0:T(8,128)S(1)}, f32[1,4,4,112,512]{4,3,2,1,0:T(8,128)S(1)}) fusion(bf16[2,4,4,112,512]{4,3,2,1,0:T(8,128)(2,1)} %shard_map.95), kind=kLoop, calls=%fused_computation.35 | loop fusion | bytes 14680064 | tf_op jit(solution)/shard_map/slice | solution.py:495
  162.1 0.0 copy-start.1
  162.1 0.0 copy-start.2
  162.1 0.0 copy-done
  162.1 3.8 %fusion.2 = bf16[1,1792,512]{2,1,0:T(8,128)(2,1)} fusion(bf16[1,4,4,112,512]{4,3,2,1,0:T(8,128)(2,1)S(1)} %copy-done, f32[1,4,4,112,512]{4,3,2,1,0:T(8,128)S(1)} %get-tuple-element.7, f32[1,4,4,112,512]{4,3,2,1,0:T(8,128)S(1)} %get-tuple-element.8), kind=kLoop, calls=%fused_computation.4 | loop fusion | flops 9175040 | bytes 11010048 | tf_op jit(solution)/shard_map/convert_element_type | solution.py:46
  165.9 0.0 copy-done.1
  165.9 0.0 copy-done.2
  (2 shorter events, 0.0 us)
Async XLA Ops:
  48.1 7.0 %copy-start.4 = (bf16[1,1,256,256]{3,2,1,0:T(8,128)(2,1)S(1)}, bf16[1,1,256,256]{3,2,1,0:T(8,128)(2,1)}, u32[]{:S(2)}) copy-start(bf16[1,1,256,256]{3,2,1,0:T(8,128)(2,1)} %param.13) | copy-start | bytes 393220
  48.1 8.8 %copy-start.3 = (bf16[2,256,1792]{2,1,0:T(8,128)(2,1)S(1)}, bf16[2,256,1792]{2,1,0:T(8,128)(2,1)}, u32[]{:S(2)}) copy-start(bf16[2,256,1792]{2,1,0:T(8,128)(2,1)} %get-tuple-element.6) | copy-start | bytes 5505028
  50.7 2.0 %collective-permute-start = (f32[256,512]{1,0:T(8,128)S(1)}, f32[256,512]{1,0:T(8,128)S(1)}, u32[]{:S(2)}, u32[]{:S(2)}) collective-permute-start(f32[256,512]{1,0:T(8,128)S(1)} %fusion.3), channel_id=1, source_target_pairs={{0,16},{16,0},{1,17},{17,1},{2,18},{18,2},{3,19},{19,3},{4,20},{20... | collective-permute-start | bytes 1572872 | tf_op jit(solution)/shard_map/ppermute | solution.py:482
  55.3 1.6 collective-permute-start.1
  158.8 3.3 %copy-start = (bf16[1,4,4,112,512]{4,3,2,1,0:T(8,128)(2,1)S(1)}, bf16[1,4,4,112,512]{4,3,2,1,0:T(8,128)(2,1)}, u32[]{:S(2)}) copy-start(bf16[1,4,4,112,512]{4,3,2,1,0:T(8,128)(2,1)} %get-tuple-element.5) | copy-start | bytes 5505028
  162.1 3.9 %copy-start.1 = (f32[1,4,4,112,512]{4,3,2,1,0:T(8,128)}, f32[1,4,4,112,512]{4,3,2,1,0:T(8,128)S(1)}, u32[]{:S(2)}) copy-start(f32[1,4,4,112,512]{4,3,2,1,0:T(8,128)S(1)} %get-tuple-element.7) | copy-start | bytes 11010052
  162.1 3.8 %copy-start.2 = (f32[1,4,4,112,512]{4,3,2,1,0:T(8,128)}, f32[1,4,4,112,512]{4,3,2,1,0:T(8,128)S(1)}, u32[]{:S(2)}) copy-start(f32[1,4,4,112,512]{4,3,2,1,0:T(8,128)S(1)} %get-tuple-element.8) | copy-start | bytes 11010052

commit v4 on v3

--- a/solution.py
+++ b/solution.py
@@ -84,7 +84,9 @@
 
 MESH = pl.DeviceIdType.MESH
 VMEM_BYTES = 60 * 1024 * 1024
-PIECES = 2
+PIECES = 3
+WEIGHT_PIECES = 2
+LEAD = 1
 
 
 def plane_size(expert_count):
@@ -119,45 +121,51 @@
     )
 
 
-def gather_kernel(channels, levels, near, with_tokens, *refs):
+def gather_kernel(cuts, levels, near, with_tokens, *refs):
+    channels = len(cuts)
+    starts = [sum(cuts[:channel]) for channel in range(channels)]
     slots = channels * (levels - 1)
     fixed = 5 if with_tokens else 3
     from_below, from_above = refs[fixed:fixed + slots], refs[fixed + slots:fixed + 2 * slots]
-    refs = refs[:fixed] + refs[fixed + 2 * slots:]
+    chosen = refs[fixed + 2 * slots:fixed + 2 * slots + channels]
+    refs = refs[:fixed] + refs[fixed + 2 * slots + channels:]
+
+    def rows(channel):
+        return pl.ds(starts[channel], cuts[channel])
 
     def slot(channel, hop):
         return channel * (levels - 1) + hop
 
     if with_tokens:
-        (place, slab, tokens, out, inputs, chosen,
+        (place, slab, tokens, out, inputs,
          up_send, up_recv, down_send, down_recv, near_send, near_recv, dp_send, dp_recv, own_sem) = refs
     else:
-        (place, slab, out, chosen,
+        (place, slab, out,
          up_send, up_recv, down_send, down_recv, near_send, near_recv) = refs
     me = lax.axis_index("expert")
     level, spot = me // near, me % near
     greet(level, levels, near, me, with_tokens)
 
     def up(channel, hop):
-        source = slab.at[channel] if hop == 0 else from_below[slot(channel, hop - 1)]
+        source = slab.at[:, rows(channel)] if hop == 0 else from_below[slot(channel, hop - 1)]
         return remote(source, from_below[slot(channel, hop)], up_send.at[channel, hop],
                       up_recv.at[channel, hop], "expert", me + near)
 
     def down(channel, hop):
-        source = slab.at[channel] if hop == 0 else from_above[slot(channel, hop - 1)]
+        source = slab.at[:, rows(channel)] if hop == 0 else from_above[slot(channel, hop - 1)]
         return remote(source, from_above[slot(channel, hop)], down_send.at[channel, hop],
                       down_recv.at[channel, hop], "expert", me - near)
 
     def across(channel, origin, step):
-        return remote(chosen.at[channel, origin, step - 1], out.at[channel, origin, spot],
+        return remote(chosen[channel].at[origin, step - 1], out.at[origin, spot, rows(channel)],
                       near_send.at[channel, origin, step - 1], near_recv.at[channel, origin, step - 1],
                       "expert", level * near + (spot ^ step))
 
     def hand_on(channel, origin, held):
         for step in range(1, near):
-            chosen[channel, origin, step - 1] = held[place[level * near + (spot ^ step)]]
+            chosen[channel][origin, step - 1] = held[place[level * near + (spot ^ step)]]
             across(channel, origin, step).start()
-        out[channel, origin, spot] = held[place[me]]
+        out[origin, spot, rows(channel), :] = held[place[me]]
 
     for channel in range(channels):
         pl.when(level < levels - 1)(lambda c=channel: up(c, 0).start())
@@ -175,7 +183,7 @@
         keep = pltpu.make_async_copy(columns(core), inputs.at[core], own_sem)
         keep.start()
     for channel in range(channels):
-        hand_on(channel, level, slab.at[channel])
+        hand_on(channel, level, slab.at[:, rows(channel)])
     for hop in range(levels - 1):
         for channel in range(channels):
 
@@ -367,12 +375,14 @@
         stage()
     for chunk in range(chunks):
         coming = stages(chunk + 1) if chunk + 1 < chunks else []
-        if coming:
-            coming[0]()
+        for stage in coming[:LEAD]:
+            stage()
         for hop in range(hops):
-            if coming:
-                coming[hop + 1]()
+            for stage in coming[LEAD + hop:LEAD + hop + 1]:
+                stage()
             forward(chunk, hop)
+        for stage in coming[LEAD + hops:]:
+            stage()
 
     for chunk in range(chunks):
         for left in range(1, levels):
@@ -387,6 +397,12 @@
                 across(chunk, goal, step).wait()
 
 
+def cut_rows(rows, pieces):
+    tiles = rows // 16
+    pieces = min(pieces, tiles)
+    return [16 * ((piece + 1) * tiles // pieces - piece * tiles // pieces) for piece in range(pieces)]
+
+
 def in_vmem():
     return pl.BlockSpec(memory_space=pltpu.VMEM)
 
@@ -395,16 +411,21 @@
     return pl.BlockSpec(memory_space=pltpu.SMEM)
 
 
-def call_gather(placement, slab, levels, near, collective_id, tokens=None):
-    channels, blocks, rows, cols = slab.shape
+def call_gather(placement, slab, levels, near, pieces, collective_id, tokens=None):
+    blocks, rows, cols = slab.shape
+    cuts = cut_rows(rows, pieces)
+    channels = len(cuts)
     kind = slab.dtype
-    out_shape = [jax.ShapeDtypeStruct((channels, levels, near, rows, cols), kind)]
+    out_shape = [jax.ShapeDtypeStruct((levels, near, rows, cols), kind)]
     in_specs = [in_smem(), in_vmem()]
     operands = [placement, slab]
     out_specs = [in_vmem()]
     dma = pltpu.SemaphoreType.DMA
-    scratch = [pltpu.VMEM((blocks, rows, cols), kind)] * (2 * channels * (levels - 1))
-    scratch += [pltpu.VMEM((channels, levels, near - 1, rows, cols), kind)]
+    scratch = []
+    for _ in range(2):
+        for cut in cuts:
+            scratch += [pltpu.VMEM((blocks, cut, cols), kind)] * (levels - 1)
+    scratch += [pltpu.VMEM((levels, near - 1, cut, cols), kind) for cut in cuts]
     scratch += [dma((channels, levels - 1))] * 4 + [dma((channels, levels, near - 1))] * 2
     if tokens is not None:
         count, width = tokens.shape
@@ -414,7 +435,7 @@
         out_specs.append(in_vmem())
         scratch += [dma, dma, dma]
     return pl.pallas_call(
-        functools.partial(gather_kernel, channels, levels, near, tokens is not None),
+        functools.partial(gather_kernel, cuts, levels, near, tokens is not None),
         out_shape=out_shape, in_specs=in_specs, out_specs=out_specs, scratch_shapes=scratch,
         compiler_params=pltpu.CompilerParams(
             collective_id=collective_id, has_side_effects=True, vmem_limit_bytes=VMEM_BYTES
@@ -426,9 +447,8 @@
     levels, near, rows, cols = term.shape
     blocks = first.shape[0]
     kind = term.dtype
-    tiles = rows // 16
-    pieces = min(pieces, tiles)
-    cuts = [16 * ((piece + 1) * tiles // pieces - piece * tiles // pieces) for piece in range(pieces)]
+    cuts = cut_rows(rows, pieces)
+    pieces = len(cuts)
     hops = levels - 1
     dma = pltpu.SemaphoreType.DMA
 
@@ -473,7 +493,9 @@
     swap = [(0, 1), (1, 0)]
     live_mask = (jnp.arange(row_total) < BLOCK * block_counts[0, 0])[:, None]
 
-    own_rows, inputs = call_gather(placement, weights[None], levels, near, 0, tokens[0, 0])
+    own_rows, inputs = call_gather(
+        placement, weights, levels, near, WEIGHT_PIECES, 0, tokens[0, 0]
+    )
     own_rows = own_rows.reshape(part_rows, col_total)
     inputs = inputs.reshape(2 * row_total, model // 2)
     mine = lax.dynamic_slice_in_dim(inputs, core * row_total, row_total)

time: 166 us -> 162 us (0.976)
  Pallas kernels: 147 us -> 143 us
    pallas_call x1, Pallas kernels: 47.4 us -> 44.1 us  [call_gather(): pl.pallas_call(functools.partial(gather_kernel, cuts, levels, near, token...]
where the time goes in v4:
time: 162 us; the launch traced here: 161 us
  Pallas kernels  143 us (88%)
  matrix products  7.36 us (5%)
  other arithmetic  3.86 us (2%)
  local copies, waits for them, and re-layouts  3.24 us (2%)
  waiting for transfers between devices  2.64 us (2%)
    pallas_call x1, Pallas kernels, call_update(): pl.pallas_call(functools.partial(update_kernel, levels, near, cuts), out_...  98.4 us
    pallas_call x1, Pallas kernels, call_gather(): pl.pallas_call(functools.partial(gather_kernel, cuts, levels, near, token...  44.1 us
    convert_element_type x1, other arithmetic, new_params(): return (params_full - learning_rate * step_size).astype(jnp.bfloat16)  3.67 us
  transfers between devices with their start and end apart: 2, of which 2 were waited for; matrix products, arithmetic and copies ran while one was open for 0% of the time, Pallas kernels for 0%

profile of v4, /device:TPU:0, one launch (start us, length us, event | category | flops | bytes accessed | tf_op | source)
XLA Modules:
  0.0 161.4 jit_solution(13781101446636881320)
XLA Ops:
  0.6 44.1 %shard_map.94 = (bf16[4,4,112,512]{3,2,1,0:T(8,128)(2,1)}, bf16[2,256,1792]{2,1,0:T(8,128)(2,1)}) custom-call(s32[16]{0:T(128)} %refs_0_.3, bf16[4,112,512]{2,1,0:T(8,128)(2,1)} %refs_1_.1, bf16[256,3584]{1,0:T(8,128)(2,1)} %bitcast.28), custom_call_target="tpu_custom_call" | custom-call | tf_op jit(solution)/shard_map/pallas_call | solution.py:437
  44.8 0.0 copy-start.4
  44.8 0.0 copy-start.3
  44.8 2.6 %fusion.3 = f32[256,512]{1,0:T(8,128)S(1)} fusion(bf16[1792,512]{1,0:T(8,128)(2,1)} %bitcast.23, bf16[512,1792]{1,0:T(8,128)(2,1)} %bitcast.29, s32[]{:T(128)S(6)} %select_n.21), kind=kOutput, calls=%fused_computation.7 | convolution fusion | flops 469762048 | bytes 3276804 | tf_op jit(solution)/shard_map/dot_general | solution.py:503
  47.4 0.1 collective-permute-start
  48.1 1.2 collective-permute-done
  49.3 2.4 %convolution_add_fusion = f32[256,512]{1,0:T(8,128)S(1)} fusion(f32[256,512]{1,0:T(8,128)S(1)} %collective-permute-done, bf16[1792,512]{1,0:T(8,128)(2,1)} %bitcast.24, bf16[512,1792]{1,0:T(8,128)(2,1)} %bitcast.30, s32[]{:T(128)S(6)} %select_n.20), kind=kOutput, calls=%fused_computation.6 | convolution fusion | flops 469893120 | bytes 3801092 | tf_op jit(solution)/shard_map/dot_general | solution.py:505
  51.8 0.0 copy-done.4
  51.8 0.2 fusion.18
  52.0 0.2 collective-permute-start.1
  52.2 1.4 collective-permute-done.1
  53.6 0.0 copy-done.3
  53.6 2.4 %bitcast_convert_fusion = bf16[1792,512]{1,0:T(8,128)(2,1)} fusion(bf16[2,256,1792]{2,1,0:T(8,128)(2,1)S(1)} %copy-done.3, bf16[1,256,512]{2,1,0:T(8,128)(2,1)S(1)} %bitcast.34, bf16[1,256,256]{2,1,0:T(8,128)(2,1)S(1)} %bitcast.33, bf16[1,256,256]{2,1,0:T(8,128)(2,1)S(1)} %bitcast.32, pred[]{:T(512)S(6)} %eq.3), kind=kOutput, calls=%fused_computation.5 | convolution fusion | flops 943849472 | bytes 4194305 | tf_op jit(solution)/shard_map/dot_general | solution.py:510
  56.0 98.4 %shard_map.95 = bf16[2,4,4,112,512]{4,3,2,1,0:T(8,128)(2,1)} custom-call(s32[16]{0:T(128)} %refs_0_.3, bf16[4,4,112,512]{3,2,1,0:T(8,128)(2,1)} %bitcast.31, f32[4,112,512]{2,1,0:T(8,128)} %refs_2_.1, f32[4,112,512]{2,1,0:T(8,128)} %refs_3_.1), custom_call_target="tpu_custom_call" | custom-call | tf_op jit(solution)/shard_map/pallas_call | solution.py:468
  154.4 0.0 copy-start
  154.4 3.2 %fusion.25 = (f32[1,4,4,112,512]{4,3,2,1,0:T(8,128)S(1)}, f32[1,4,4,112,512]{4,3,2,1,0:T(8,128)S(1)}) fusion(bf16[2,4,4,112,512]{4,3,2,1,0:T(8,128)(2,1)} %shard_map.95), kind=kLoop, calls=%fused_computation.35 | loop fusion | bytes 14680064 | tf_op jit(solution)/shard_map/slice | solution.py:517
  157.6 0.0 copy-start.1
  157.7 0.0 copy-start.2
  157.7 0.0 copy-done
  157.7 3.7 %fusion.2 = bf16[1,1792,512]{2,1,0:T(8,128)(2,1)} fusion(bf16[1,1792,512]{2,1,0:T(8,128)(2,1)S(1)} %bitcast.25, f32[1,4,4,112,512]{4,3,2,1,0:T(8,128)S(1)} %get-tuple-element.7, f32[1,4,4,112,512]{4,3,2,1,0:T(8,128)S(1)} %get-tuple-element.8), kind=kLoop, calls=%fused_computation.4 | loop fusion | flops 9175040 | bytes 11010048 | tf_op jit(solution)/shard_map/convert_element_type | solution.py:46
  161.3 0.0 copy-done.1
  161.4 0.0 copy-done.2
  (2 shorter events, 0.0 us)
Async XLA Ops:
  44.8 7.0 %copy-start.4 = (bf16[1,1,256,256]{3,2,1,0:T(8,128)(2,1)S(1)}, bf16[1,1,256,256]{3,2,1,0:T(8,128)(2,1)}, u32[]{:S(2)}) copy-start(bf16[1,1,256,256]{3,2,1,0:T(8,128)(2,1)} %param.13) | copy-start | bytes 393220
  44.8 8.8 %copy-start.3 = (bf16[2,256,1792]{2,1,0:T(8,128)(2,1)S(1)}, bf16[2,256,1792]{2,1,0:T(8,128)(2,1)}, u32[]{:S(2)}) copy-start(bf16[2,256,1792]{2,1,0:T(8,128)(2,1)} %get-tuple-element.6) | copy-start | bytes 5505028
  47.4 2.0 %collective-permute-start = (f32[256,512]{1,0:T(8,128)S(1)}, f32[256,512]{1,0:T(8,128)S(1)}, u32[]{:S(2)}, u32[]{:S(2)}) collective-permute-start(f32[256,512]{1,0:T(8,128)S(1)} %fusion.3), channel_id=1, source_target_pairs={{0,16},{16,0},{1,17},{17,1},{2,18},{18,2},{3,19},{19,3},{4,20},{20... | collective-permute-start | bytes 1572872 | tf_op jit(solution)/shard_map/ppermute | solution.py:504
  52.0 1.6 collective-permute-start.1
  154.4 3.3 %copy-start = (bf16[4,4,112,512]{3,2,1,0:T(8,128)(2,1)S(1)}, bf16[4,4,112,512]{3,2,1,0:T(8,128)(2,1)}, u32[]{:S(2)}) copy-start(bf16[4,4,112,512]{3,2,1,0:T(8,128)(2,1)} %get-tuple-element.5) | copy-start | bytes 5505028
  157.6 3.7 %copy-start.1 = (f32[1,4,4,112,512]{4,3,2,1,0:T(8,128)}, f32[1,4,4,112,512]{4,3,2,1,0:T(8,128)S(1)}, u32[]{:S(2)}) copy-start(f32[1,4,4,112,512]{4,3,2,1,0:T(8,128)S(1)} %get-tuple-element.7) | copy-start | bytes 11010052
  157.7 3.7 %copy-start.2 = (f32[1,4,4,112,512]{4,3,2,1,0:T(8,128)}, f32[1,4,4,112,512]{4,3,2,1,0:T(8,128)S(1)}, u32[]{:S(2)}) copy-start(f32[1,4,4,112,512]{4,3,2,1,0:T(8,128)S(1)} %get-tuple-element.8) | copy-start | bytes 11010052

commit v5 on v4

--- a/solution.py
+++ b/solution.py
@@ -400,7 +400,9 @@
 def cut_rows(rows, pieces):
     tiles = rows // 16
     pieces = min(pieces, tiles)
-    return [16 * ((piece + 1) * tiles // pieces - piece * tiles // pieces) for piece in range(pieces)]
+    fullest = sorted(range(pieces), key=lambda piece: (piece == pieces - 1, piece == 0))
+    extra = fullest[: tiles % pieces]
+    return [16 * (tiles // pieces + int(piece in extra)) for piece in range(pieces)]
 
 
 def in_vmem():

time: 162 us -> 161 us (level)
  no operation moved by 1% of the time
where the time goes in v5:
time: 161 us; the launch traced here: 160 us
  Pallas kernels  142 us (88%)
  matrix products  7.36 us (5%)
  other arithmetic  3.86 us (2%)
  local copies, waits for them, and re-layouts  3.24 us (2%)
  waiting for transfers between devices  2.64 us (2%)
    pallas_call x1, Pallas kernels, call_update(): pl.pallas_call(functools.partial(update_kernel, levels, near, cuts), out_...  97.8 us
    pallas_call x1, Pallas kernels, call_gather(): pl.pallas_call(functools.partial(gather_kernel, cuts, levels, near, token...  43.8 us
    convert_element_type x1, other arithmetic, new_params(): return (params_full - learning_rate * step_size).astype(jnp.bfloat16)  3.67 us
  transfers between devices with their start and end apart: 2, of which 2 were waited for; matrix products, arithmetic and copies ran while one was open for 0% of the time, Pallas kernels for 0%

profile of v5, /device:TPU:0, one launch (start us, length us, event | category | flops | bytes accessed | tf_op | source)
XLA Modules:
  0.0 160.4 jit_solution(10430993762654390850)
XLA Ops:
  0.6 43.8 %shard_map.94 = (bf16[4,4,112,512]{3,2,1,0:T(8,128)(2,1)}, bf16[2,256,1792]{2,1,0:T(8,128)(2,1)}) custom-call(s32[16]{0:T(128)} %refs_0_.3, bf16[4,112,512]{2,1,0:T(8,128)(2,1)} %refs_1_.1, bf16[256,3584]{1,0:T(8,128)(2,1)} %bitcast.28), custom_call_target="tpu_custom_call" | custom-call | tf_op jit(solution)/shard_map/pallas_call | solution.py:439
  44.4 0.0 copy-start.4
  44.4 0.0 copy-start.3
  44.4 2.6 %fusion.3 = f32[256,512]{1,0:T(8,128)S(1)} fusion(bf16[1792,512]{1,0:T(8,128)(2,1)} %bitcast.23, bf16[512,1792]{1,0:T(8,128)(2,1)} %bitcast.29, s32[]{:T(128)S(6)} %select_n.21), kind=kOutput, calls=%fused_computation.7 | convolution fusion | flops 469762048 | bytes 3276804 | tf_op jit(solution)/shard_map/dot_general | solution.py:505
  47.0 0.1 collective-permute-start
  47.7 1.2 collective-permute-done
  49.0 2.4 %convolution_add_fusion = f32[256,512]{1,0:T(8,128)S(1)} fusion(f32[256,512]{1,0:T(8,128)S(1)} %collective-permute-done, bf16[1792,512]{1,0:T(8,128)(2,1)} %bitcast.24, bf16[512,1792]{1,0:T(8,128)(2,1)} %bitcast.30, s32[]{:T(128)S(6)} %select_n.20), kind=kOutput, calls=%fused_computation.6 | convolution fusion | flops 469893120 | bytes 3801092 | tf_op jit(solution)/shard_map/dot_general | solution.py:507
  51.4 0.0 copy-done.4
  51.4 0.2 fusion.18
  51.6 0.2 collective-permute-start.1
  51.8 1.4 collective-permute-done.1
  53.2 0.0 copy-done.3
  53.2 2.4 %bitcast_convert_fusion = bf16[1792,512]{1,0:T(8,128)(2,1)} fusion(bf16[2,256,1792]{2,1,0:T(8,128)(2,1)S(1)} %copy-done.3, bf16[1,256,512]{2,1,0:T(8,128)(2,1)S(1)} %bitcast.34, bf16[1,256,256]{2,1,0:T(8,128)(2,1)S(1)} %bitcast.33, bf16[1,256,256]{2,1,0:T(8,128)(2,1)S(1)} %bitcast.32, pred[]{:T(512)S(6)} %eq.3), kind=kOutput, calls=%fused_computation.5 | convolution fusion | flops 943849472 | bytes 4194305 | tf_op jit(solution)/shard_map/dot_general | solution.py:512
  55.6 97.8 %shard_map.95 = bf16[2,4,4,112,512]{4,3,2,1,0:T(8,128)(2,1)} custom-call(s32[16]{0:T(128)} %refs_0_.3, bf16[4,4,112,512]{3,2,1,0:T(8,128)(2,1)} %bitcast.31, f32[4,112,512]{2,1,0:T(8,128)} %refs_2_.1, f32[4,112,512]{2,1,0:T(8,128)} %refs_3_.1), custom_call_target="tpu_custom_call" | custom-call | tf_op jit(solution)/shard_map/pallas_call | solution.py:470
  153.4 0.0 copy-start
  153.4 3.2 %fusion.25 = (f32[1,4,4,112,512]{4,3,2,1,0:T(8,128)S(1)}, f32[1,4,4,112,512]{4,3,2,1,0:T(8,128)S(1)}) fusion(bf16[2,4,4,112,512]{4,3,2,1,0:T(8,128)(2,1)} %shard_map.95), kind=kLoop, calls=%fused_computation.35 | loop fusion | bytes 14680064 | tf_op jit(solution)/shard_map/slice | solution.py:519
  156.7 0.0 copy-start.1
  156.7 0.0 copy-start.2
  156.7 0.0 copy-done
  156.7 3.7 %fusion.2 = bf16[1,1792,512]{2,1,0:T(8,128)(2,1)} fusion(bf16[1,1792,512]{2,1,0:T(8,128)(2,1)S(1)} %bitcast.25, f32[1,4,4,112,512]{4,3,2,1,0:T(8,128)S(1)} %get-tuple-element.7, f32[1,4,4,112,512]{4,3,2,1,0:T(8,128)S(1)} %get-tuple-element.8), kind=kLoop, calls=%fused_computation.4 | loop fusion | flops 9175040 | bytes 11010048 | tf_op jit(solution)/shard_map/convert_element_type | solution.py:46
  160.4 0.0 copy-done.1
  160.4 0.0 copy-done.2
  (2 shorter events, 0.0 us)
Async XLA Ops:
  44.4 7.0 %copy-start.4 = (bf16[1,1,256,256]{3,2,1,0:T(8,128)(2,1)S(1)}, bf16[1,1,256,256]{3,2,1,0:T(8,128)(2,1)}, u32[]{:S(2)}) copy-start(bf16[1,1,256,256]{3,2,1,0:T(8,128)(2,1)} %param.13) | copy-start | bytes 393220
  44.4 8.8 %copy-start.3 = (bf16[2,256,1792]{2,1,0:T(8,128)(2,1)S(1)}, bf16[2,256,1792]{2,1,0:T(8,128)(2,1)}, u32[]{:S(2)}) copy-start(bf16[2,256,1792]{2,1,0:T(8,128)(2,1)} %get-tuple-element.6) | copy-start | bytes 5505028
  47.0 2.0 %collective-permute-start = (f32[256,512]{1,0:T(8,128)S(1)}, f32[256,512]{1,0:T(8,128)S(1)}, u32[]{:S(2)}, u32[]{:S(2)}) collective-permute-start(f32[256,512]{1,0:T(8,128)S(1)} %fusion.3), channel_id=1, source_target_pairs={{0,16},{16,0},{1,17},{17,1},{2,18},{18,2},{3,19},{19,3},{4,20},{20... | collective-permute-start | bytes 1572872 | tf_op jit(solution)/shard_map/ppermute | solution.py:506
  51.6 1.6 collective-permute-start.1
  153.4 3.3 %copy-start = (bf16[4,4,112,512]{3,2,1,0:T(8,128)(2,1)S(1)}, bf16[4,4,112,512]{3,2,1,0:T(8,128)(2,1)}, u32[]{:S(2)}) copy-start(bf16[4,4,112,512]{3,2,1,0:T(8,128)(2,1)} %get-tuple-element.5) | copy-start | bytes 5505028
  156.7 3.7 %copy-start.1 = (f32[1,4,4,112,512]{4,3,2,1,0:T(8,128)}, f32[1,4,4,112,512]{4,3,2,1,0:T(8,128)S(1)}, u32[]{:S(2)}) copy-start(f32[1,4,4,112,512]{4,3,2,1,0:T(8,128)S(1)} %get-tuple-element.7) | copy-start | bytes 11010052
  156.7 3.7 %copy-start.2 = (f32[1,4,4,112,512]{4,3,2,1,0:T(8,128)}, f32[1,4,4,112,512]{4,3,2,1,0:T(8,128)S(1)}, u32[]{:S(2)}) copy-start(f32[1,4,4,112,512]{4,3,2,1,0:T(8,128)S(1)} %get-tuple-element.8) | copy-start | bytes 11010052
